TPU v7x, 32 devices: a whole 2x2x4 slice. The times are simulated.
32 devices in a mesh: grp: 2 (over y), tok: 4 (over z), sec: 2 (over core), ch: 2 (over x).
Axes of the slice: x: 2, y: 2, z: 4, core: 2. Of those that a mesh axis runs over, the one named last changes fastest.
Arguments:
- features: bfloat16 [4096, 2048], P('ch', ('grp', 'tok', 'sec')), parts along dimension 1, may hold values from -6 to 6
- gate_one: bfloat16 [4096, 2048], P('ch', ('grp', 'tok', 'sec')), parts along dimension 1, may hold values from -6 to 6
- taps_one: bfloat16 [4096, 128], P('ch'), may hold values from -0.5 to 0.5
- long_filter: bfloat16 [4096, 1024], P('ch', ('tok', 'sec')), may hold values from -0.1875 to 0.1875
- skip_gain: float32 [4096], P('ch'), may hold values from 0.5 to 1.5
- taps_two: bfloat16 [4096, 128], P('ch'), may hold values from -0.5 to 0.5
- gate_two: bfloat16 [4096, 2048], P('ch', ('grp', 'tok', 'sec')), parts along dimension 1, may hold values from -6 to 6
Outputs:
- mixed_out: bfloat16 [4096, 2048], P('ch', ('grp', 'tok', 'sec')), parts along dimension 1
There are 2 independent parts, one for each index of `grp`. A program takes and returns all parts, laid end to end along the dimension named above; an argument that names none is the same for every part. Nothing has to cross between parts.
All inputs are finite; a program needn't handle non-finite values.
Results may differ from a plain program's by a relative error of at most 0.0057.
Values may be sent and summed in bfloat16 or wider, within the bound.
No kernel may reach another device: no remote copies, remote signals or barrier semaphores. Data moves between devices by JAX's collectives and lax.ppermute only.
A program may use at most 192 MiB of HBM per device.

v0:
```python
import math

import jax
import jax.numpy as jnp
from jax import lax
from jax.sharding import PartitionSpec as P


def passed_along(array, axis, by):
    length = lax.axis_size(axis)
    pairs = [(i, i + by) for i in range(length) if 0 <= i + by < length]
    return lax.ppermute(array, axis, pairs)


def depthwise(padded, kernel_taps):
    tap_count = kernel_taps.shape[1]
    length = padded.shape[1] - (tap_count - 1)
    group_size = 16
    total = jnp.zeros((padded.shape[0], length), jnp.float32)
    for first in range(0, tap_count, group_size):
        last = min(first + group_size, tap_count)
        stacked = jnp.stack(
            [padded[:, tap_count - 1 - k : tap_count - 1 - k + length] for k in range(first, last)],
            axis=1,
        )
        total = total + jnp.einsum(
            "cgl,cg->cl", stacked, kernel_taps[:, first:last], preferred_element_type=jnp.float32
        )
    return total


def angle_table(rows_count, cols_count, period):
    row_index = jnp.arange(rows_count, dtype=jnp.int32)[:, None]
    col_index = jnp.arange(cols_count, dtype=jnp.int32)[None, :]
    phase = (row_index * col_index % period).astype(jnp.float32) * (2.0 * math.pi / period)
    return (jnp.cos(phase), jnp.sin(phase))


def contract(form, left, right):
    return jnp.einsum(form, left, right, precision=lax.Precision.HIGHEST)


def forward_spectrum(signal, outer, inner, total):
    half_outer = outer // 2
    cos_first, sin_first = angle_table(half_outer, outer, outer)
    turn_cos, turn_sin = angle_table(outer, inner, total)
    cos_inner, sin_inner = angle_table(inner, inner, inner)
    shaped = signal.reshape(signal.shape[0], half_outer, inner)
    real_a = contract("cmn,mk->ckn", shaped, cos_first)
    imag_a = -contract("cmn,mk->ckn", shaped, sin_first)
    real_b = real_a * turn_cos + imag_a * turn_sin
    imag_b = imag_a * turn_cos - real_a * turn_sin
    real_c = contract("ckn,nj->cjk", real_b, cos_inner) + contract("ckn,nj->cjk", imag_b, sin_inner)
    imag_c = contract("ckn,nj->cjk", imag_b, cos_inner) - contract("ckn,nj->cjk", real_b, sin_inner)
    return (real_c, imag_c)


def inverse_spectrum(real_y, imag_y, outer, inner, total):
    half_outer = outer // 2
    cos_inner, sin_inner = angle_table(inner, inner, inner)
    turn_cos, turn_sin = angle_table(outer, inner, total)
    cos_last, sin_last = angle_table(outer, half_outer, outer)
    real_c = contract("cjk,jn->ckn", real_y, cos_inner) - contract("cjk,jn->ckn", imag_y, sin_inner)
    imag_c = contract("cjk,jn->ckn", imag_y, cos_inner) + contract("cjk,jn->ckn", real_y, sin_inner)
    real_d = real_c * turn_cos - imag_c * turn_sin
    imag_d = imag_c * turn_cos + real_c * turn_sin
    result = contract("ckn,km->cmn", real_d, cos_last) - contract("ckn,km->cmn", imag_d, sin_last)
    return (result / total).reshape(real_y.shape[0], half_outer * inner)


def on_device(features, gate_one, taps_one, long_filter, skip_gain, taps_two, gate_two):
    shards = lax.axis_size(("tok", "sec"))
    channels, block_len = features.shape
    narrow = channels // shards
    seq_len = block_len * shards
    rim_width = taps_one.shape[1] - 1
    total = 2 * seq_len
    inner = math.gcd(seq_len, 128)
    outer = total // inner
    filter_rows = lax.all_to_all(
        long_filter[:, None, :], ("tok", "sec"), split_axis=0, concat_axis=1, tiled=True
    ).reshape(narrow, seq_len)
    rim_rows = passed_along(features[:, block_len - rim_width :], ("tok", "sec"), 1)
    first_conv = depthwise(jnp.concatenate([rim_rows, features], axis=1), taps_one)
    mixed_one = (first_conv * gate_one).astype(jnp.bfloat16)
    channel_rows = lax.all_to_all(
        mixed_one[:, None, :], ("tok", "sec"), split_axis=0, concat_axis=1, tiled=True
    )
    channel_rows = channel_rows.reshape(narrow, seq_len).astype(jnp.float32)
    filter_real, filter_imag = forward_spectrum(
        filter_rows.astype(jnp.float32), outer, inner, total
    )
    signal_real, signal_imag = forward_spectrum(channel_rows, outer, inner, total)
    product_real = signal_real * filter_real - signal_imag * filter_imag
    product_imag = signal_real * filter_imag + signal_imag * filter_real
    conv_rows = inverse_spectrum(product_real, product_imag, outer, inner, total)
    skip_local = lax.dynamic_slice_in_dim(
        skip_gain, lax.axis_index(("tok", "sec")) * narrow, narrow
    )
    long_out = (conv_rows + skip_local[:, None] * channel_rows).astype(jnp.bfloat16)
    long_blocks = long_out.reshape(narrow, shards, block_len)
    tail_rows = jnp.concatenate(
        [
            jnp.zeros((narrow, 1, rim_width), jnp.bfloat16),
            long_blocks[:, :-1, block_len - rim_width :],
        ],
        axis=1,
    )
    windows = jnp.concatenate([tail_rows, long_blocks], axis=2)
    padded = lax.all_to_all(
        windows, ("tok", "sec"), split_axis=1, concat_axis=0, tiled=True
    ).reshape(channels, block_len + rim_width)
    second_conv = depthwise(padded, taps_two)
    return (second_conv * gate_two).astype(jnp.bfloat16)


def solution(mesh):
    in_specs = (
        P("ch", ("grp", "tok", "sec")),
        P("ch", ("grp", "tok", "sec")),
        P("ch", None),
        P("ch", ("tok", "sec")),
        P("ch"),
        P("ch", None),
        P("ch", ("grp", "tok", "sec")),
    )
    out_specs = P("ch", ("grp", "tok", "sec"))
    return jax.shard_map(
        on_device, mesh=mesh, in_specs=in_specs, out_specs=out_specs, check_vma=False
    )
```

profile of v0, /device:TPU:0, one launch (start us, length us, event | category | flops | bytes accessed | tf_op | source)
XLA Modules:
  0.0 428.2 jit_solution(18028862349489927458)
XLA Ops:
  8.2 6.1 %all-to-all-start.1 = ((bf16[8,2,16384]{2,1,0:T(2,128)(2,1)}), bf16[8,2,16384]{2,1,0:T(2,128)(2,1)S(1)}, u32[]{:S(2)}, u32[]{:S(2)}) async-start(bf16[8,2,16384]{2,1,0:T(2,128)(2,1)} %reshape.112), calls=%async_computation.1 | async-start | bytes 1048576 | tf_op jit(solution)/shard_map/all_to_all | solution.py:80
  14.3 5.7 %slice_bitcast_fusion.142 = (bf16[2048,16,1]{1,0,2:T(8,128)(2,1)S(1)}, bf16[2048,16,1]{1,0,2:T(8,128)(2,1)}, bf16[2048,16,1]{1,0,2:T(8,128)(2,1)}, bf16[2048,16,...) fusion(bf16[2048,128]{1,0:T(8,128)(2,1)} %param.9), kind=kLoop, calls=%fused_computation.1013 | loop fusion | bytes 1048576 | tf_op jit(solution)/shard_map/slice | solution.py:27
  28.0 3.2 copy-done.13
  31.2 3.5 constant_dynamic-update-slice_fusion.16
  50.5 3.0 constant_dynamic-update-slice_fusion
  59.8 3.5 constant_dynamic-update-slice_fusion.32
  69.1 2.8 constant_dynamic-update-slice_fusion.48
  110.5 8.7 %fusion.16 = f32[2048,1,128]{2,1,0:T(1,128)S(1)} fusion(bf16[2048,16,128]{2,0,1:T(8,128)(2,1)} %constant_dynamic-update-slice_fusion.112, bf16[2048,16,1]{1,0,2:T(8,128)(2,1)S(1)} %get-tuple-element.191), kind=kOutput, calls=%fused_computation.268 | convolution fusion | flops 8388608 | bytes 9502720 | tf_op jit(solution)/shard_map/cgl,cg->cl/dot_general | solution.py:26
  119.2 8.7 %fusion.18 = f32[2048,1,128]{2,1,0:T(1,128)S(1)} fusion(bf16[2048,16,128]{2,0,1:T(8,128)(2,1)} %get-tuple-element.175, bf16[2048,16,1]{1,0,2:T(8,128)(2,1)S(1)} %get-tuple-element.192), kind=kOutput, calls=%fused_computation.270 | convolution fusion | flops 8388608 | bytes 9502720 | tf_op jit(solution)/shard_map/cgl,cg->cl/dot_general | solution.py:26
  128.0 9.2 %fusion.20 = f32[2048,1,128]{2,1,0:T(1,128)S(1)} fusion(bf16[2048,16,128]{2,0,1:T(8,128)(2,1)} %copy-done.9, bf16[2048,16,1]{1,0,2:T(8,128)(2,1)} %get-tuple-element.186), kind=kOutput, calls=%fused_computation.272 | convolution fusion | flops 8388608 | bytes 9502720 | tf_op jit(solution)/shard_map/cgl,cg->cl/dot_general | solution.py:26
  137.1 9.8 %fusion.22 = f32[2048,1,128]{2,1,0:T(1,128)} fusion(bf16[2048,16,128]{2,0,1:T(8,128)(2,1)} %copy-done.8, bf16[2048,16,1]{1,0,2:T(8,128)(2,1)} %get-tuple-element.187), kind=kOutput, calls=%fused_computation.274 | convolution fusion | flops 8388608 | bytes 9502720 | tf_op jit(solution)/shard_map/cgl,cg->cl/dot_general | solution.py:26
  146.9 10.0 %fusion.24 = f32[2048,1,128]{2,1,0:T(1,128)} fusion(bf16[2048,16,128]{2,0,1:T(8,128)(2,1)} %copy-done.7, bf16[2048,16,1]{1,0,2:T(8,128)(2,1)} %get-tuple-element.188), kind=kOutput, calls=%fused_computation.276 | convolution fusion | flops 8388608 | bytes 9502720 | tf_op jit(solution)/shard_map/cgl,cg->cl/dot_general | solution.py:26
  156.9 9.8 %fusion.26 = f32[2048,1,128]{2,1,0:T(1,128)} fusion(bf16[2048,16,128]{2,0,1:T(8,128)(2,1)} %copy-done.6, bf16[2048,16,1]{1,0,2:T(8,128)(2,1)} %get-tuple-element.189), kind=kOutput, calls=%fused_computation.278 | convolution fusion | flops 8388608 | bytes 9502720 | tf_op jit(solution)/shard_map/cgl,cg->cl/dot_general | solution.py:26
  166.6 10.1 %fusion.30 = f32[2048,1,128]{2,1,0:T(1,128)} fusion(bf16[2048,16,128]{2,0,1:T(8,128)(2,1)} %get-tuple-element.149, bf16[2048,16,1]{1,0,2:T(8,128)(2,1)S(1)} %get-tuple-element.190), kind=kOutput, calls=%fused_computation.282 | convolution fusion | flops 8388608 | bytes 9502720 | tf_op jit(solution)/shard_map/cgl,cg->cl/dot_general | solution.py:26
  176.7 9.8 %fusion.28 = f32[2048,1,128]{2,1,0:T(1,128)} fusion(bf16[2048,16,128]{2,0,1:T(8,128)(2,1)} %get-tuple-element.141, bf16[2048,16,1]{1,0,2:T(8,128)(2,1)S(1)} %get-tuple-element.185), kind=kOutput, calls=%fused_computation.280 | convolution fusion | flops 8388608 | bytes 9502720 | tf_op jit(solution)/shard_map/cgl,cg->cl/dot_general | solution.py:26
  186.5 2.9 fusion.111
  191.4 5.1 %all-to-all-start = ((bf16[8,2,16384]{2,1,0:T(2,128)(2,1)}), bf16[8,2,16384]{2,1,0:T(2,128)(2,1)}, u32[]{:S(2)}, u32[]{:S(2)}) async-start(bf16[8,2,16384]{2,1,0:T(2,128)(2,1)} %reshape.110), calls=%async_computation | async-start | bytes 1048576 | tf_op jit(solution)/shard_map/all_to_all | solution.py:86
  199.1 2.4 fusion.367
  201.5 10.4 %all-to-all-done = bf16[8,2,16384]{2,1,0:T(2,128)(2,1)} async-done(((bf16[8,2,16384]{2,1,0:T(2,128)(2,1)}), bf16[8,2,16384]{2,1,0:T(2,128)(2,1)}, u32[]{:S(2)}, u32[]{:S(2)}) %all-to-all-start) | async-done | bytes 524320 | tf_op jit(solution)/shard_map/all_to_all | solution.py:86
  215.5 3.5 add_bitcast_fusion
  219.1 2.6 fusion.47
  221.7 2.6 fusion.45
  224.3 2.6 fusion.55
  226.9 2.8 fusion.53
  229.7 2.7 fusion.67
  232.4 2.7 fusion.70
  235.2 2.7 fusion.61
  237.9 3.5 multiply_subtract_fusion.1
  241.4 3.6 fusion.34
  245.0 3.6 fusion.32
  248.6 3.7 fusion.73
  252.3 3.8 multiply_subtract_fusion
  258.4 2.6 fusion.91
  263.0 3.8 all-to-all-start.2
  266.8 2.7 slice_bitcast_fusion.134
  269.5 23.6 %all-to-all-done.2 = bf16[256,8,255]{2,0,1:T(8,128)(2,1)S(1)} async-done(((bf16[256,8,255]{2,0,1:T(8,128)(2,1)}), bf16[256,8,255]{2,0,1:T(8,128)(2,1)S(1)}, u32[]{:S(2)}, u32[]{:S(2)}) %all-to-all-start.2) | async-done | bytes 1044512 | tf_op jit(solution)/shard_map/all_to_all | solution.py:110
  293.1 2.8 constant_dynamic-update-slice_fusion.159
  295.8 3.0 constant_dynamic-update-slice_fusion.158
  298.9 3.0 constant_dynamic-update-slice_fusion.157
  301.9 3.0 constant_dynamic-update-slice_fusion.156
  304.9 3.0 constant_dynamic-update-slice_fusion.155
  307.9 3.1 constant_dynamic-update-slice_fusion.154
  311.0 3.0 constant_dynamic-update-slice_fusion.153
  313.9 3.0 constant_dynamic-update-slice_fusion.152
  317.0 3.1 constant_dynamic-update-slice_fusion.151
  320.0 3.4 constant_dynamic-update-slice_fusion.150
  323.4 3.0 constant_dynamic-update-slice_fusion.149
  326.4 3.1 constant_dynamic-update-slice_fusion.148
  329.5 3.0 constant_dynamic-update-slice_fusion.147
  332.5 3.0 constant_dynamic-update-slice_fusion.146
  335.5 3.0 constant_dynamic-update-slice_fusion.145
  338.5 2.8 constant_dynamic-update-slice_fusion.144
  341.4 3.2 copy-done.10
  344.6 2.6 copy-done.11
  347.2 2.4 copy-done.12
  349.6 8.9 %fusion.14 = f32[2048,1,128]{2,1,0:T(1,128)S(1)} fusion(bf16[2048,16,128]{2,0,1:T(8,128)(2,1)} %get-tuple-element.20, bf16[2048,16,1]{1,0,2:T(8,128)(2,1)S(1)} %copy-done.5), kind=kOutput, calls=%fused_computation.266 | convolution fusion | flops 8388608 | bytes 9502720 | tf_op jit(solution)/shard_map/cgl,cg->cl/dot_general | solution.py:26
  358.5 8.7 %fusion.12 = f32[2048,1,128]{2,1,0:T(1,128)S(1)} fusion(bf16[2048,16,128]{2,0,1:T(8,128)(2,1)} %copy-done.10, bf16[2048,16,1]{1,0,2:T(8,128)(2,1)S(1)} %copy-done.4), kind=kOutput, calls=%fused_computation.264 | convolution fusion | flops 8388608 | bytes 9502720 | tf_op jit(solution)/shard_map/cgl,cg->cl/dot_general | solution.py:26
  367.2 8.9 %fusion.10 = f32[2048,1,128]{2,1,0:T(1,128)S(1)} fusion(bf16[2048,16,128]{2,0,1:T(8,128)(2,1)} %get-tuple-element.19, bf16[2048,16,1]{1,0,2:T(8,128)(2,1)S(1)} %get-tuple-element.181), kind=kOutput, calls=%fused_computation.262 | convolution fusion | flops 8388608 | bytes 9502720 | tf_op jit(solution)/shard_map/cgl,cg->cl/dot_general | solution.py:26
  376.2 8.8 %fusion.8 = f32[2048,1,128]{2,1,0:T(1,128)S(1)} fusion(bf16[2048,16,128]{2,0,1:T(8,128)(2,1)} %get-tuple-element.18, bf16[2048,16,1]{1,0,2:T(8,128)(2,1)} %get-tuple-element.180), kind=kOutput, calls=%fused_computation.260 | convolution fusion | flops 8388608 | bytes 9502720 | tf_op jit(solution)/shard_map/cgl,cg->cl/dot_general | solution.py:26
  384.9 10.1 %fusion.6 = f32[2048,1,128]{2,1,0:T(1,128)} fusion(bf16[2048,16,128]{2,0,1:T(8,128)(2,1)} %get-tuple-element.17, bf16[2048,16,1]{1,0,2:T(8,128)(2,1)} %get-tuple-element.179), kind=kOutput, calls=%fused_computation.258 | convolution fusion | flops 8388608 | bytes 9502720 | tf_op jit(solution)/shard_map/cgl,cg->cl/dot_general | solution.py:26
  395.0 9.8 %fusion.4 = f32[2048,1,128]{2,1,0:T(1,128)} fusion(bf16[2048,16,128]{2,0,1:T(8,128)(2,1)} %get-tuple-element.16, bf16[2048,16,1]{1,0,2:T(8,128)(2,1)} %get-tuple-element.178), kind=kOutput, calls=%fused_computation.256 | convolution fusion | flops 8388608 | bytes 9502720 | tf_op jit(solution)/shard_map/cgl,cg->cl/dot_general | solution.py:26
  404.8 9.7 %fusion.2 = f32[2048,1,128]{2,1,0:T(1,128)} fusion(bf16[2048,16,128]{2,0,1:T(8,128)(2,1)} %copy-done.12, bf16[2048,16,1]{1,0,2:T(8,128)(2,1)S(1)} %get-tuple-element.184), kind=kOutput, calls=%fused_computation.254 | convolution fusion | flops 8388608 | bytes 9502720 | tf_op jit(solution)/shard_map/cgl,cg->cl/dot_general | solution.py:26
  414.5 10.0 %fusion = f32[2048,1,128]{2,1,0:T(1,128)} fusion(bf16[2048,16,128]{2,0,1:T(8,128)(2,1)} %copy-done.11, bf16[2048,16,1]{1,0,2:T(8,128)(2,1)} %get-tuple-element.183), kind=kOutput, calls=%fused_computation.252 | convolution fusion | flops 8388608 | bytes 9502720 | tf_op jit(solution)/shard_map/cgl,cg->cl/dot_general | solution.py:26
  424.5 3.6 multiply_convert_fusion
  (140 shorter events, 94.9 us)
Async XLA Ops:
  0.0 20.0 %copy-start = (bf16[2048,128]{1,0:T(8,128)(2,1)S(1)}, bf16[2048,128]{1,0:T(8,128)(2,1)}, u32[]{:S(2)}) copy-start(bf16[2048,128]{1,0:T(8,128)(2,1)} %param.7) | copy-start | bytes 1572868
  2.1 17.9 %collective-permute-start = (bf16[2048,127]{1,0:T(8,128)(2,1)}, bf16[2048,127]{1,0:T(8,128)(2,1)S(1)}, u32[]{:S(2)}, u32[]{:S(2)}) collective-permute-start(bf16[2048,127]{1,0:T(8,128)(2,1)} %slice.819), channel_id=1, source_target_pairs={{0,2},{2,4},{4,6},{6,8},{8,10},{10,12},{12,14},{1,3},{3,5},{5,7},{... | collective-permute-start | bytes 1560584 | tf_op jit(solution)/shard_map/ppermute | solution.py:12
  8.2 183.3 %all-to-all-start.1 = ((bf16[8,2,16384]{2,1,0:T(2,128)(2,1)}), bf16[8,2,16384]{2,1,0:T(2,128)(2,1)S(1)}, u32[]{:S(2)}, u32[]{:S(2)}) async-start(bf16[8,2,16384]{2,1,0:T(2,128)(2,1)} %reshape.112), calls=%async_computation.1 | async-start | bytes 1048576 | tf_op jit(solution)/shard_map/all_to_all | solution.py:80
  28.0 3.2 copy-start.13
  63.3 5.3 %copy-start.6 = (bf16[2048,16,128]{2,0,1:T(8,128)(2,1)}, bf16[2048,16,128]{2,0,1:T(8,128)(2,1)S(1)}, u32[]{:S(2)}) copy-start(bf16[2048,16,128]{2,0,1:T(8,128)(2,1)S(1)} %get-tuple-element.157) | copy-start | bytes 25165828
  71.9 5.3 %copy-start.7 = (bf16[2048,16,128]{2,0,1:T(8,128)(2,1)}, bf16[2048,16,128]{2,0,1:T(8,128)(2,1)S(1)}, u32[]{:S(2)}) copy-start(bf16[2048,16,128]{2,0,1:T(8,128)(2,1)S(1)} %get-tuple-element.163) | copy-start | bytes 25165828
  79.6 7.1 %copy-start.8 = (bf16[2048,16,128]{2,0,1:T(8,128)(2,1)}, bf16[2048,16,128]{2,0,1:T(8,128)(2,1)S(1)}, u32[]{:S(2)}) copy-start(bf16[2048,16,128]{2,0,1:T(8,128)(2,1)S(1)} %get-tuple-element.168) | copy-start | bytes 25165828
  86.7 14.3 %copy-start.9 = (bf16[2048,16,128]{2,0,1:T(8,128)(2,1)}, bf16[2048,16,128]{2,0,1:T(8,128)(2,1)S(1)}, u32[]{:S(2)}) copy-start(bf16[2048,16,128]{2,0,1:T(8,128)(2,1)S(1)} %get-tuple-element.172) | copy-start | bytes 25165828
  176.7 9.8 %copy-start.2 = (bf16[2048,128]{1,0:T(8,128)(2,1)S(1)}, bf16[2048,128]{1,0:T(8,128)(2,1)}, u32[]{:S(2)}) copy-start(bf16[2048,128]{1,0:T(8,128)(2,1)} %param.8) | copy-start | bytes 1572868
  191.4 20.5 %all-to-all-start = ((bf16[8,2,16384]{2,1,0:T(2,128)(2,1)}), bf16[8,2,16384]{2,1,0:T(2,128)(2,1)}, u32[]{:S(2)}, u32[]{:S(2)}) async-start(bf16[8,2,16384]{2,1,0:T(2,128)(2,1)} %reshape.110), calls=%async_computation | async-start | bytes 1048576 | tf_op jit(solution)/shard_map/all_to_all | solution.py:86
  256.1 10.7 %copy-start.1 = (bf16[2048,128]{1,0:T(8,128)(2,1)S(1)}, bf16[2048,128]{1,0:T(8,128)(2,1)}, u32[]{:S(2)}) copy-start(bf16[2048,128]{1,0:T(8,128)(2,1)} %param.12) | copy-start | bytes 1572868
  263.0 30.1 %all-to-all-start.2 = ((bf16[256,8,255]{2,0,1:T(8,128)(2,1)}), bf16[256,8,255]{2,0,1:T(8,128)(2,1)S(1)}, u32[]{:S(2)}, u32[]{:S(2)}) async-start(bf16[256,8,255]{2,0,1:T(8,128)(2,1)} %copy.106), calls=%async_computation.2 | async-start | bytes 2097152 | tf_op jit(solution)/shard_map/all_to_all | solution.py:110
  335.5 14.1 %copy-start.5 = (bf16[2048,16,1]{1,0,2:T(8,128)(2,1)S(1)}, bf16[2048,16,1]{1,0,2:T(8,128)(2,1)}, u32[]{:S(2)}) copy-start(bf16[2048,16,1]{1,0,2:T(8,128)(2,1)} %get-tuple-element.182) | copy-start | bytes 196612
  341.3 3.2 copy-start.10
  341.4 5.8 %copy-start.11 = (bf16[2048,16,128]{2,0,1:T(8,128)(2,1)}, bf16[2048,16,128]{2,0,1:T(8,128)(2,1)S(1)}, u32[]{:S(2)}) copy-start(bf16[2048,16,128]{2,0,1:T(8,128)(2,1)S(1)} %get-tuple-element.14) | copy-start | bytes 25165828
  341.4 8.2 %copy-start.12 = (bf16[2048,16,128]{2,0,1:T(8,128)(2,1)}, bf16[2048,16,128]{2,0,1:T(8,128)(2,1)S(1)}, u32[]{:S(2)}) copy-start(bf16[2048,16,128]{2,0,1:T(8,128)(2,1)S(1)} %get-tuple-element.15) | copy-start | bytes 25165828
  341.4 17.1 %copy-start.4 = (bf16[2048,16,1]{1,0,2:T(8,128)(2,1)S(1)}, bf16[2048,16,1]{1,0,2:T(8,128)(2,1)}, u32[]{:S(2)}) copy-start(bf16[2048,16,1]{1,0,2:T(8,128)(2,1)} %get-tuple-element.177) | copy-start | bytes 196612
  414.5 10.0 %copy-start.3 = (bf16[2048,128]{1,0:T(8,128)(2,1)S(1)}, bf16[2048,128]{1,0:T(8,128)(2,1)}, u32[]{:S(2)}) copy-start(bf16[2048,128]{1,0:T(8,128)(2,1)} %param.13) | copy-start | bytes 1572868
where the time goes:
time: 436 us; the launch traced here: 428 us
  matrix products  201 us (46%)
  other arithmetic  97.4 us (22%)
  local copies, waits for them, and re-layouts  78 us (18%)
  waiting for transfers between devices  34 us (8%)
  starting transfers between devices  17.4 us (4%)
    dot_general x16, matrix products, depthwise(): jnp.einsum('cgl,cg->cl', stacked, kernel_taps[:, first:last], preferred_e...  151 us
    unnamed x91, other arithmetic  67.3 us
    unnamed x49, local copies, waits for them, and re-layouts  61.9 us
    dot_general x18, matrix products, contract(): return jnp.einsum(form, left, right, precision=lax.Precision.HIGHEST)  50 us
    all_to_all x1, waiting for transfers between devices, on_device(): lax.all_to_all(windows, ('tok', 'sec'), split_axis=1, concat_axis=0, tile...  23.6 us
    another operation x8, other arithmetic, depthwise(): jnp.stack([padded[:, tap_count - 1 - k:tap_count - 1 - k + length] for k...  19.8 us
    all_to_all x1, waiting for transfers between devices, on_device(): lax.all_to_all(mixed_one[:, None, :], ('tok', 'sec'), split_axis=0, conca...  10.4 us
  transfers between devices with their start and end apart: 4, of which 2 were waited for; matrix products, arithmetic and copies ran while one was open for 43% of the time, Pallas kernels for 0%

commit v1 on v0

v1 whole, which is shorter than its diff:
```python
import functools
import math

import jax
import jax.numpy as jnp
import numpy as np
from jax import lax
from jax.experimental import pallas as pl
from jax.experimental.pallas import tpu as pltpu
from jax.sharding import PartitionSpec as P

AXES = ("tok", "sec")
F32 = jnp.float32
BF16 = jnp.bfloat16


def split_const(matrix):
    hi = matrix.astype(np.float32).astype(jnp.bfloat16)
    lo = (matrix - hi.astype(np.float64)).astype(np.float32).astype(jnp.bfloat16)
    return hi, lo


def tables(block):
    length = 2 * block
    sample = np.arange(length)[:, None]
    freq = np.arange(block)[None, :]
    turns = (sample * (2 * freq + 1)) % (2 * length)
    angle = turns * (math.pi / length)
    forward = np.concatenate([np.cos(angle), -np.sin(angle)], axis=1)
    hi, lo = split_const(forward)
    top = np.concatenate([hi[:block], lo[:block]], axis=0)
    back = forward[block:].T / block
    back_hi, back_lo = split_const(back)
    both = np.concatenate([back_hi, back_lo], axis=1)
    return tuple(jnp.asarray(t) for t in (hi, lo, top, both))


def mm(left, right):
    return jnp.dot(left, right, preferred_element_type=F32)


def window_spectrum(before, here, hi, lo):
    window = jnp.concatenate([before, here], axis=1)
    return mm(window, hi) + mm(window, lo)


def block_spectrum(rows, top):
    return mm(jnp.concatenate([rows, rows], axis=1), top)


def two_parts(value):
    hi = value.astype(BF16)
    return hi, (value - hi.astype(F32)).astype(BF16)


def times(left, right):
    n = left.shape[-1] // 2
    lr, li, rr, ri = left[:, :n], left[:, n:], right[:, :n], right[:, n:]
    return jnp.concatenate([lr * rr - li * ri, lr * ri + li * rr], axis=1)


def valid_part(spectrum, both):
    n = both.shape[1] // 2
    hi, lo = two_parts(spectrum)
    wide = mm(hi, both)
    return wide[:, :n] + wide[:, n:] + mm(lo, both[:, :n])


def rows_at(index, rows):
    return pl.ds(pl.multiple_of(index * rows, rows), rows)


def first_kernel(shards, me_ref, x_ref, halo_ref, gate_ref, taps_ref, hi_ref, lo_ref, top_ref, both_ref, *outs):
    rows = outs[0].shape[0]
    me = me_ref[0]
    hi, lo, top, both = hi_ref[...], lo_ref[...], top_ref[...], both_ref[...]
    for k in range(shards):
        at = rows_at(me ^ k, rows)
        spectrum = window_spectrum(halo_ref[at, :], x_ref[at, :], hi, lo)
        taps = block_spectrum(taps_ref[at, :], top)
        conv = valid_part(times(spectrum, taps), both)
        outs[k][...] = (conv * gate_ref[at, :].astype(F32)).astype(BF16)


def filter_kernel(shards, me_ref, mine_ref, other_ref, taps_ref, skip_ref, hi_ref, lo_ref, top_ref, both_ref, out_ref, lags, taps_hat):
    half = mine_ref.shape[1]
    me, group = me_ref[0], me_ref[1]
    hi, lo, top, both = hi_ref[...], lo_ref[...], top_ref[...], both_ref[...]
    lags[0] = jnp.zeros(lags.shape[1:], BF16)
    for k in range(shards):
        lags[(me ^ k) + 1, rows_at(group, half), :] = mine_ref[k]
        lags[(me ^ k) + 1, rows_at(1 - group, half), :] = other_ref[k]
    taps_hat[...] = block_spectrum(taps_ref[...], top)
    for m in range(shards):
        spectrum = window_spectrum(lags[m], lags[m + 1], hi, lo)
        joined = valid_part(times(spectrum, taps_hat[...]), both)
        part_hi, part_lo = two_parts(joined)
        n = part_hi.shape[1]
        result = block_spectrum(part_hi, top) + mm(part_lo, top[:n])
        if m == 0:
            result = result + skip_ref[...] * taps_hat[...]
        out_ref[m] = result


def long_kernel(shards, me_ref, *refs):
    pieces = refs[:shards]
    filt_ref, hi_ref, lo_ref, both_ref = refs[shards : shards + 4]
    outs = refs[shards + 4 : 2 * shards + 4]
    signal, spectra, sums = refs[2 * shards + 4 :]
    rows, block = pieces[0].shape
    me = me_ref[0]
    hi, lo, both = hi_ref[...], lo_ref[...], both_ref[...]
    signal[0] = jnp.zeros((rows, block), BF16)
    for k in range(shards):
        signal[(me ^ k) + 1] = pieces[k][...]
    for j in range(shards):
        spectra[j] = window_spectrum(signal[j], signal[j + 1], hi, lo)
    tile = 8

    def body(i, carry):
        at = pl.ds(pl.multiple_of(i * tile, tile), tile)
        fr = [filt_ref[m, at, :block] for m in range(shards)]
        fi = [filt_ref[m, at, block:] for m in range(shards)]
        sr = [spectra[m, at, :block] for m in range(shards)]
        si = [spectra[m, at, block:] for m in range(shards)]
        for j in range(shards):
            re = fr[0] * sr[j] - fi[0] * si[j]
            im = fr[0] * si[j] + fi[0] * sr[j]
            for m in range(1, j + 1):
                re = re + (fr[m] * sr[j - m] - fi[m] * si[j - m])
                im = im + (fr[m] * si[j - m] + fi[m] * sr[j - m])
            sums[j, at, :block] = re
            sums[j, at, block:] = im
        return carry

    lax.fori_loop(0, rows // tile, body, 0)
    for k in range(shards):
        outs[k][...] = valid_part(sums[me ^ k], both).astype(BF16)


def last_kernel(shards, me_ref, *refs):
    pieces, gate_ref, out_ref = refs[:shards], refs[shards], refs[shards + 1]
    rows = pieces[0].shape[0]
    me = me_ref[0]
    for k in range(shards):
        at = rows_at(me ^ k, rows)
        out_ref[at, :] = (pieces[k][...].astype(F32) * gate_ref[at, :].astype(F32)).astype(BF16)


def call(kernel, inputs, out_shape, scratch=(), flops=0, name=None):
    vmem = pl.BlockSpec(memory_space=pltpu.VMEM)
    many = isinstance(out_shape, (list, tuple))
    moved = sum(math.prod(a.shape) * a.dtype.itemsize for a in inputs)
    return pl.pallas_call(
        kernel,
        out_shape=out_shape,
        in_specs=[pl.BlockSpec(memory_space=pltpu.SMEM)] + [vmem] * (len(inputs) - 1),
        out_specs=[vmem] * len(out_shape) if many else vmem,
        scratch_shapes=list(scratch),
        compiler_params=pltpu.CompilerParams(vmem_limit_bytes=28 * 1024 * 1024),
        cost_estimate=pl.CostEstimate(flops=flops, bytes_accessed=moved, transcendentals=0),
        name=name,
    )(*inputs)


def on_device(features, gate_one, taps_one, long_filter, skip_gain, taps_two, gate_two):
    shards = lax.axis_size(AXES)
    groups = lax.axis_size("grp")
    assert shards & (shards - 1) == 0 and groups == 2
    channels, block = features.shape
    assert taps_one.shape[1] == block and taps_two.shape[1] == block
    narrow = channels // shards
    half = narrow // groups
    hi, lo, top, both = tables(block)
    me = lax.axis_index(AXES)
    group = lax.axis_index("grp")
    place = jnp.stack([me, group]).astype(jnp.int32)
    flops = 2 * channels * 256 * 256

    def swapped(piece, k):
        return lax.ppermute(piece, AXES, [(i, i ^ k) for i in range(shards)])

    halo = lax.ppermute(features, AXES, [(i, i + 1) for i in range(shards - 1)])

    by_owner = long_filter.reshape(shards, groups, half, block)
    lags = [
        lax.dynamic_slice(by_owner, (me ^ k, group, 0, 0), (1, 1, half, block)).reshape(half, block)
        for k in range(shards)
    ]
    lags = [lags[0]] + [swapped(lags[k], k) for k in range(1, shards)]
    mine = jnp.stack(lags)
    other = lax.ppermute(mine, "grp", [(0, 1), (1, 0)])

    piece = jax.ShapeDtypeStruct((narrow, block), BF16)
    mixed = call(
        functools.partial(first_kernel, shards),
        (place, features, halo, gate_one, taps_one, hi, lo, top, both),
        [piece] * shards,
        flops=6 * flops,
        name="first",
    )
    mixed = [mixed[0]] + [swapped(mixed[k], k) for k in range(1, shards)]

    taps_local = lax.dynamic_slice_in_dim(taps_two, me * narrow, narrow)
    skip_local = lax.dynamic_slice_in_dim(skip_gain, me * narrow, narrow)[:, None]
    joined = call(
        functools.partial(filter_kernel, shards),
        (place, mine, other, taps_local, skip_local, hi, lo, top, both),
        jax.ShapeDtypeStruct((shards, narrow, 2 * block), F32),
        scratch=[
            pltpu.VMEM((shards + 1, narrow, block), BF16),
            pltpu.VMEM((narrow, 2 * block), F32),
        ],
        flops=6 * flops,
        name="filter",
    )
    result = call(
        functools.partial(long_kernel, shards),
        (place, *mixed, joined, hi, lo, both),
        [piece] * shards,
        scratch=[
            pltpu.VMEM((shards + 1, narrow, block), BF16),
            pltpu.VMEM((shards, narrow, 2 * block), F32),
            pltpu.VMEM((shards, narrow, 2 * block), F32),
        ],
        flops=6 * flops,
        name="long",
    )
    result = [result[0]] + [swapped(result[k], k) for k in range(1, shards)]
    return call(
        functools.partial(last_kernel, shards),
        (place, *result, gate_two),
        jax.ShapeDtypeStruct((channels, block), BF16),
        flops=channels * block,
        name="last",
    )


def solution(mesh):
    in_specs = (
        P("ch", ("grp", "tok", "sec")),
        P("ch", ("grp", "tok", "sec")),
        P("ch", None),
        P("ch", ("tok", "sec")),
        P("ch"),
        P("ch", None),
        P("ch", ("grp", "tok", "sec")),
    )
    out_specs = P("ch", ("grp", "tok", "sec"))
    return jax.shard_map(
        on_device, mesh=mesh, in_specs=in_specs, out_specs=out_specs, check_vma=False
    )
```

time: 436 us -> 70.3 us (0.16); the launches traced: 428 us -> 69.3 us
  matrix products: 201 us -> 0 us
  other arithmetic: 97.4 us -> 0.07 us
  local copies, waits for them, and re-layouts: 78 us -> 9.42 us
  waiting for transfers between devices: 34 us -> 13 us
  starting transfers between devices: 17.4 us -> 35.6 us
  Pallas kernels: 0 us -> 11 us
    dot_general x34 -> x0, matrix products: 201 us -> none  [the longest x16 151 us: depthwise(): jnp.einsum('cgl,cg->cl', stacked, kernel_taps[:, first:last], preferred_e...]
    unnamed x91 -> x0, other arithmetic: 67.3 us -> none
    unnamed x49 -> x33, local copies, waits for them, and re-layouts: 61.9 us -> 7.58 us
    all_to_all x3 -> x0, waiting for transfers between devices: 34 us -> none  [the longest x1 23.6 us: on_device(): lax.all_to_all(windows, ('tok', 'sec'), split_axis=1, concat_axis=0, tile...]
    ppermute x1 -> x23, starting transfers between devices: 2.42 us -> 35.6 us  [the longest x21 31.9 us: swapped(): return lax.ppermute(piece, AXES, [(i, i ^ k) for i in range(shards)])]
    another operation x8 -> x1, other arithmetic: 19.8 us -> 0.07 us  [on_device(): place = jnp.stack([me, group]).astype(jnp.int32)]
    all_to_all x3 -> x0, starting transfers between devices: 15 us -> none  [the longest x1 6.12 us: on_device(): lax.all_to_all(long_filter[:, None, :], ('tok', 'sec'), split_axis=0, con...]
    ppermute x1 -> x23, waiting for transfers between devices: 0.01 us -> 13 us  [the longest x21 13 us: swapped(): return lax.ppermute(piece, AXES, [(i, i ^ k) for i in range(shards)])]
  transfers between devices with their start and end apart: 4 -> 23, of which waited for: 2 -> 3; matrix products, arithmetic and copies ran while one was open for 43% -> 3% of each run, Pallas kernels for 0% -> 9%
where the time goes in v1:
time: 70.3 us; the launch traced here: 69.3 us
  starting transfers between devices  35.6 us (51%)
  waiting for transfers between devices  13 us (18%)
  Pallas kernels  11 us (16%)
  local copies, waits for them, and re-layouts  9.42 us (13%)
    ppermute x21, starting transfers between devices, swapped(): return lax.ppermute(piece, AXES, [(i, i ^ k) for i in range(shards)])  31.9 us
    ppermute x21, waiting for transfers between devices, swapped(): return lax.ppermute(piece, AXES, [(i, i ^ k) for i in range(shards)])  13 us
    pallas_call x4, Pallas kernels, call(): pl.pallas_call(kernel, out_shape=out_shape, in_specs=[pl.BlockSpec(memory...  11 us
    unnamed x33, local copies, waits for them, and re-layouts  7.58 us
    ppermute x1, starting transfers between devices, on_device(): halo = lax.ppermute(features, AXES, [(i, i + 1) for i in range(shards - 1)])  2.2 us
    ppermute x1, starting transfers between devices, on_device(): other = lax.ppermute(mine, 'grp', [(0, 1), (1, 0)])  1.52 us
  transfers between devices with their start and end apart: 23, of which 3 were waited for; matrix products, arithmetic and copies ran while one was open for 3% of the time, Pallas kernels for 9%

profile of v1, /device:TPU:0, one launch (start us, length us, event | category | flops | bytes accessed | tf_op | source)
XLA Modules:
  0.0 69.3 jit_solution(9774596550328078211)
XLA Ops:
  0.0 0.0 copy-start
  0.0 0.9 %dynamic-slice_bitcast_fusion = (bf16[128,128]{1,0:T(8,128)(2,1)S(1)}, bf16[128,128]{1,0:T(8,128)(2,1)S(1)}, bf16[128,128]{1,0:T(8,128)(2,1)S(1)}, bf16[128,128]...) fusion(bf16[8,2,128,128]{3,2,1,0:T(8,128)(2,1)} %bitcast.34, ...), kind=kLoop, calls=%fused_computation.8 | loop fusion | bytes 458784 | tf_op jit(solution)/shard_map/reshape | solution.py:187
  0.9 0.6 collective-permute-start.8
  1.5 2.6 %collective-permute-start.9 = (bf16[128,128]{1,0:T(8,128)(2,1)S(1)}, bf16[128,128]{1,0:T(8,128)(2,1)S(1)}, u32[]{:S(2)}, u32[]{:S(2)}) collective-permute-start(bf16[128,128]{1,0:T(8,128)(2,1)S(1)} %get-tuple-element.42), channel_id=1, source_target_pairs={{0,4},{2,6},{4,0},{6,2},{8,12},{10,14},{12,8},{14,10},{1,5},{3,7},... | collective-permute-start | bytes 98312 | tf_op jit(solution)/shard_map/ppermute | solution.py:181
  4.1 0.0 collective-permute-start.10
  4.2 2.8 %collective-permute-start.11 = (bf16[128,128]{1,0:T(8,128)(2,1)S(1)}, bf16[128,128]{1,0:T(8,128)(2,1)S(1)}, u32[]{:S(2)}, u32[]{:S(2)}) collective-permute-start(bf16[128,128]{1,0:T(8,128)(2,1)S(1)} %get-tuple-element.40), channel_id=1, source_target_pairs={{0,8},{2,10},{4,12},{6,14},{8,0},{10,2},{12,4},{14,6},{1,9},{3,11}... | collective-permute-start | bytes 98312 | tf_op jit(solution)/shard_map/ppermute | solution.py:181
  6.9 0.0 collective-permute-start.12
  6.9 0.8 %bitcast_dynamic-update-slice_fusion.7 = bf16[8,128,128]{2,1,0:T(8,128)(2,1)S(1)} fusion(bf16[8,2,128,128]{3,2,1,0:T(8,128)(2,1)} %bitcast.35, s32[]{:T(128)S(6)} %select_n.38, s32[]{:T(128)S(6)} %select_n.39), kind=kLoop, calls=%fused_computation.7 | loop fusion | bytes 65544
  7.7 0.1 pad_add_fusion.me_ref
  7.8 0.8 %dynamic_slice.39 = f32[256]{0:T(256)S(1)} dynamic-slice(f32[2048]{0:T(1024)} %param.15, s32[]{:T(128)S(6)} %select_n.47), dynamic_slice_sizes={256} | dynamic-slice | bytes 2052 | tf_op jit(solution)/shard_map/dynamic_slice | solution.py:205
  8.5 0.1 copy.12.skip_ref
  8.7 0.0 collective-permute-done.8
  8.7 3.7 %collective-permute-start.13 = (bf16[128,128]{1,0:T(8,128)(2,1)S(1)}, bf16[128,128]{1,0:T(8,128)(2,1)S(1)}, u32[]{:S(2)}, u32[]{:S(2)}) collective-permute-start(bf16[128,128]{1,0:T(8,128)(2,1)S(1)} %get-tuple-element.38), channel_id=1, source_target_pairs={{0,12},{2,14},{4,8},{6,10},{8,4},{10,6},{12,0},{14,2},{1,13},{3,15... | collective-permute-start | bytes 98312 | tf_op jit(solution)/shard_map/ppermute | solution.py:181
  12.4 0.0 collective-permute-done.9
  12.4 0.1 collective-permute-start.14
  12.5 0.0 collective-permute-done.10
  12.5 2.2 %collective-permute-start = (bf16[2048,128]{1,0:T(8,128)(2,1)}, bf16[2048,128]{1,0:T(8,128)(2,1)S(1)}, u32[]{:S(2)}, u32[]{:S(2)}) collective-permute-start(bf16[2048,128]{1,0:T(8,128)(2,1)} %x_ref.1), channel_id=1, source_target_pairs={{0,2},{2,4},{4,6},{6,8},{8,10},{10,12},{12,14},{1,3},{3,5},{5,7},{... | collective-permute-start | bytes 1572872 | tf_op jit(solution)/shard_map/ppermute | solution.py:183
  14.7 0.0 collective-permute-done.11
  14.8 0.0 collective-permute-done.12
  14.8 0.0 collective-permute-done.13
  14.8 2.8 %collective-permute-done.14 = bf16[128,128]{1,0:T(8,128)(2,1)S(1)} collective-permute-done((bf16[128,128]{1,0:T(8,128)(2,1)S(1)}, bf16[128,128]{1,0:T(8,128)(2,1)S(1)}, u32[]{:S(2)}, u32[]{:S(2)}) %collective-permute-start.14) | collective-permute-done | bytes 32800 | tf_op jit(solution)/shard_map/ppermute | solution.py:181
  17.6 1.5 %collective-permute-start.15 = (bf16[8,128,128]{2,1,0:T(8,128)(2,1)S(1)}, bf16[8,128,128]{2,1,0:T(8,128)(2,1)S(1)}, u32[]{:S(2)}, u32[]{:S(2)}) collective-permute-start(bf16[8,128,128]{2,1,0:T(8,128)(2,1)S(1)} %bitcast_dynamic-update-slice_fusion.mine_ref), channel_id=1, source_target_pairs={{0,16},{16,0},{1,17},{17,1},{2,18},{18,2},{3,19},{19,3},{4,20},{20... | collective-permute-start | bytes 786440 | tf_op jit(solution)/shard_map/ppermute | solution.py:192
  19.1 0.0 collective-permute-done.halo_ref
  19.1 1.0 %copy-done.2 = bf16[2048,128]{1,0:T(8,128)(2,1)S(1)} copy-done((bf16[2048,128]{1,0:T(8,128)(2,1)S(1)}, bf16[2048,128]{1,0:T(8,128)(2,1)}, u32[]{:S(2)}) %copy-start.2) | copy-done | bytes 524312
  20.2 1.0 %copy-done.3 = bf16[2048,128]{1,0:T(8,128)(2,1)S(1)} copy-done((bf16[2048,128]{1,0:T(8,128)(2,1)S(1)}, bf16[2048,128]{1,0:T(8,128)(2,1)}, u32[]{:S(2)}) %copy-start.3) | copy-done | bytes 524312
  21.2 1.0 %copy-done.4 = bf16[2048,128]{1,0:T(8,128)(2,1)S(1)} copy-done((bf16[2048,128]{1,0:T(8,128)(2,1)S(1)}, bf16[2048,128]{1,0:T(8,128)(2,1)}, u32[]{:S(2)}) %copy-start.4) | copy-done | bytes 524312
  22.3 0.9 %copy-done.5 = bf16[256,256]{1,0:T(8,128)(2,1)S(1)} copy-done((bf16[256,256]{1,0:T(8,128)(2,1)S(1)}, bf16[256,256]{1,0:T(8,128)(2,1)}, u32[]{:S(2)}) %copy-start.5) | copy-done | bytes 131096
  23.2 0.9 %copy-done.7 = bf16[256,256]{1,0:T(8,128)(2,1)S(1)} copy-done((bf16[256,256]{1,0:T(8,128)(2,1)S(1)}, bf16[256,256]{1,0:T(8,128)(2,1)}, u32[]{:S(2)}) %copy-start.7) | copy-done | bytes 131096
  24.1 0.9 %copy-done.9 = bf16[256,256]{1,0:T(8,128)(2,1)S(1)} copy-done((bf16[256,256]{1,0:T(8,128)(2,1)S(1)}, bf16[256,256]{1,0:T(8,128)(2,1)}, u32[]{:S(2)}) %copy-start.9) | copy-done | bytes 131096
  25.0 0.9 %copy-done.11 = bf16[256,256]{1,0:T(8,128)(2,1)S(1)} copy-done((bf16[256,256]{1,0:T(8,128)(2,1)S(1)}, bf16[256,256]{1,0:T(8,128)(2,1)}, u32[]{:S(2)}) %copy-start.11) | copy-done | bytes 131096
  25.9 3.0 %first.1 = (bf16[256,128]{1,0:T(8,128)(2,1)S(1)}, bf16[256,128]{1,0:T(8,128)(2,1)S(1)}, bf16[256,128]{1,0:T(8,128)(2,1)S(1)}, bf16[256,128]{1,0:T(8,128)(2,1)S(1...) custom-call(s32[2]{0:T(128)S(1)} %pad_add_fusion.me_ref, ...), custom_call_target="tpu_custom_call" | custom-call | flops 1610612736 | bytes 2621448 | tf_op jit(solution)/shard_map/first/pallas_call | solution.py:154
  28.9 2.1 %collective-permute-start.1 = (bf16[256,128]{1,0:T(8,128)(2,1)S(1)}, bf16[256,128]{1,0:T(8,128)(2,1)S(1)}, u32[]{:S(2)}, u32[]{:S(2)}) collective-permute-start(bf16[256,128]{1,0:T(8,128)(2,1)S(1)} %get-tuple-element.22), channel_id=1, source_target_pairs={{0,2},{2,0},{4,6},{6,4},{8,10},{10,8},{12,14},{14,12},{1,3},{3,1},... | collective-permute-start | bytes 196616 | tf_op jit(solution)/shard_map/ppermute | solution.py:181
  31.0 2.3 %collective-permute-start.2 = (bf16[256,128]{1,0:T(8,128)(2,1)S(1)}, bf16[256,128]{1,0:T(8,128)(2,1)S(1)}, u32[]{:S(2)}, u32[]{:S(2)}) collective-permute-start(bf16[256,128]{1,0:T(8,128)(2,1)S(1)} %get-tuple-element.23), channel_id=1, source_target_pairs={{0,4},{2,6},{4,0},{6,2},{8,12},{10,14},{12,8},{14,10},{1,5},{3,7},... | collective-permute-start | bytes 196616 | tf_op jit(solution)/shard_map/ppermute | solution.py:181
  33.3 0.1 collective-permute-start.3
  33.4 4.0 %collective-permute-start.4 = (bf16[256,128]{1,0:T(8,128)(2,1)S(1)}, bf16[256,128]{1,0:T(8,128)(2,1)S(1)}, u32[]{:S(2)}, u32[]{:S(2)}) collective-permute-start(bf16[256,128]{1,0:T(8,128)(2,1)S(1)} %get-tuple-element.25), channel_id=1, source_target_pairs={{0,8},{2,10},{4,12},{6,14},{8,0},{10,2},{12,4},{14,6},{1,9},{3,11}... | collective-permute-start | bytes 196616 | tf_op jit(solution)/shard_map/ppermute | solution.py:181
  37.4 0.0 collective-permute-done.15.other_ref
  37.4 0.0 collective-permute-start.5
  37.4 0.0 collective-permute-done.1.refs_1_
  37.4 3.7 %collective-permute-start.6 = (bf16[256,128]{1,0:T(8,128)(2,1)S(1)}, bf16[256,128]{1,0:T(8,128)(2,1)S(1)}, u32[]{:S(2)}, u32[]{:S(2)}) collective-permute-start(bf16[256,128]{1,0:T(8,128)(2,1)S(1)} %get-tuple-element.27), channel_id=1, source_target_pairs={{0,12},{2,14},{4,8},{6,10},{8,4},{10,6},{12,0},{14,2},{1,13},{3,15... | collective-permute-start | bytes 196616 | tf_op jit(solution)/shard_map/ppermute | solution.py:181
  41.1 0.0 collective-permute-done.2.refs_2_
  41.1 0.1 collective-permute-start.7
  41.3 0.0 copy-done.10
  41.3 3.1 %filter.1.refs_8_ = f32[8,256,256]{2,1,0:T(8,128)S(1)} custom-call(s32[2]{0:T(128)S(1)} %pad_add_fusion.me_ref, bf16[8,128,128]{2,1,0:T(8,128)(2,1)S(1)} %bitcast_dynamic-update-slice_fusion.mine_ref, bf16[8,128,128]{2,1,0:T(8,128)(2,1)S(1)} %collective-permute-done.15.other_ref, bf16[256,128]{1,0:T(8,128)(2,1)S(1)} %constant_dynamic-slice_fusion.taps_ref, ...), custom_call_target="tpu_custom_call" | custom-call | flops 1610612736 | bytes 1115144 | tf_op jit(solution)/shard_map/filter/pallas_call | solution.py:154
  44.4 0.0 collective-permute-done.3.refs_3_
  44.4 0.0 collective-permute-done.4.refs_4_
  44.4 3.6 %collective-permute-done.5.refs_5_ = bf16[256,128]{1,0:T(8,128)(2,1)S(1)} collective-permute-done((bf16[256,128]{1,0:T(8,128)(2,1)S(1)}, bf16[256,128]{1,0:T(8,128)(2,1)S(1)}, u32[]{:S(2)}, u32[]{:S(2)}) %collective-permute-start.5) | collective-permute-done | bytes 65568 | tf_op jit(solution)/shard_map/ppermute | solution.py:181
  48.0 0.0 collective-permute-done.6.refs_6_
  48.0 0.0 collective-permute-done.7.refs_7_
  48.0 3.4 %long.1 = (bf16[256,128]{1,0:T(8,128)(2,1)S(1)}, bf16[256,128]{1,0:T(8,128)(2,1)S(1)}, bf16[256,128]{1,0:T(8,128)(2,1)S(1)}, bf16[256,128]{1,0:T(8,128)(2,1)S(1)...) custom-call(s32[2]{0:T(128)S(1)} %pad_add_fusion.me_ref, ...), custom_call_target="tpu_custom_call" | custom-call | flops 1610612736 | bytes 3014664 | tf_op jit(solution)/shard_map/long/pallas_call | solution.py:154
  51.5 0.2 collective-permute-start.16
  51.6 3.4 %collective-permute-start.17 = (bf16[256,128]{1,0:T(8,128)(2,1)S(1)}, bf16[256,128]{1,0:T(8,128)(2,1)S(1)}, u32[]{:S(2)}, u32[]{:S(2)}) collective-permute-start(bf16[256,128]{1,0:T(8,128)(2,1)S(1)} %get-tuple-element.31), channel_id=1, source_target_pairs={{0,4},{2,6},{4,0},{6,2},{8,12},{10,14},{12,8},{14,10},{1,5},{3,7},... | collective-permute-start | bytes 196616 | tf_op jit(solution)/shard_map/ppermute | solution.py:181
  55.0 0.0 collective-permute-start.18
  55.0 2.5 %collective-permute-start.19 = (bf16[256,128]{1,0:T(8,128)(2,1)S(1)}, bf16[256,128]{1,0:T(8,128)(2,1)S(1)}, u32[]{:S(2)}, u32[]{:S(2)}) collective-permute-start(bf16[256,128]{1,0:T(8,128)(2,1)S(1)} %get-tuple-element.33), channel_id=1, source_target_pairs={{0,8},{2,10},{4,12},{6,14},{8,0},{10,2},{12,4},{14,6},{1,9},{3,11}... | collective-permute-start | bytes 196616 | tf_op jit(solution)/shard_map/ppermute | solution.py:181
  57.5 0.0 collective-permute-start.20
  57.5 0.0 collective-permute-done.16.refs_1_
  57.5 2.1 %collective-permute-start.21 = (bf16[256,128]{1,0:T(8,128)(2,1)S(1)}, bf16[256,128]{1,0:T(8,128)(2,1)S(1)}, u32[]{:S(2)}, u32[]{:S(2)}) collective-permute-start(bf16[256,128]{1,0:T(8,128)(2,1)S(1)} %get-tuple-element.35), channel_id=1, source_target_pairs={{0,12},{2,14},{4,8},{6,10},{8,4},{10,6},{12,0},{14,2},{1,13},{3,15... | collective-permute-start | bytes 196616 | tf_op jit(solution)/shard_map/ppermute | solution.py:181
  59.7 0.0 collective-permute-done.17.refs_2_
  59.7 1.5 %collective-permute-start.22 = (bf16[256,128]{1,0:T(8,128)(2,1)S(1)}, bf16[256,128]{1,0:T(8,128)(2,1)S(1)}, u32[]{:S(2)}, u32[]{:S(2)}) collective-permute-start(bf16[256,128]{1,0:T(8,128)(2,1)S(1)} %get-tuple-element.36), channel_id=1, source_target_pairs={{0,14},{2,12},{4,10},{6,8},{8,6},{10,4},{12,2},{14,0},{1,15},{3,13... | collective-permute-start | bytes 196616 | tf_op jit(solution)/shard_map/ppermute | solution.py:181
  61.2 0.0 collective-permute-done.18.refs_3_
  61.2 0.0 collective-permute-done.19.refs_4_
  61.2 6.6 %collective-permute-done.20.refs_5_ = bf16[256,128]{1,0:T(8,128)(2,1)S(1)} collective-permute-done((bf16[256,128]{1,0:T(8,128)(2,1)S(1)}, bf16[256,128]{1,0:T(8,128)(2,1)S(1)}, u32[]{:S(2)}, u32[]{:S(2)}) %collective-permute-start.20) | collective-permute-done | bytes 65568 | tf_op jit(solution)/shard_map/ppermute | solution.py:181
  67.8 0.0 collective-permute-done.21.refs_6_
  67.8 0.0 collective-permute-done.22.refs_7_
  67.8 1.5 %last.1 = bf16[2048,128]{1,0:T(8,128)(2,1)} custom-call(s32[2]{0:T(128)S(1)} %pad_add_fusion.me_ref, bf16[256,128]{1,0:T(8,128)(2,1)S(1)} %get-tuple-element.29.refs_0_, bf16[256,128]{1,0:T(8,128)(2,1)S(1)} %collective-permute-done.16.refs_1_, bf16[256,128]{1,0:T(8,128)(2,1)S(1)} %collective-permute-done.17.refs_2_, ...), custom_call_target="tpu_custom_call" | custom-call | flops 262144 | bytes 1048584 | tf_op jit(solution)/shard_map/last/pallas_call | solution.py:154
  (25 shorter events, 0.1 us)
Async XLA Ops:
  0.0 33.3 %copy-start = (bf16[2048,128]{1,0:T(8,128)(2,1)S(1)}, bf16[2048,128]{1,0:T(8,128)(2,1)}, u32[]{:S(2)}) copy-start(bf16[2048,128]{1,0:T(8,128)(2,1)} %param.16) | copy-start | bytes 1572868
  0.9 7.7 %collective-permute-start.8 = (bf16[128,128]{1,0:T(8,128)(2,1)S(1)}, bf16[128,128]{1,0:T(8,128)(2,1)S(1)}, u32[]{:S(2)}, u32[]{:S(2)}) collective-permute-start(bf16[128,128]{1,0:T(8,128)(2,1)S(1)} %get-tuple-element.43), channel_id=1, source_target_pairs={{0,2},{2,0},{4,6},{6,4},{8,10},{10,8},{12,14},{14,12},{1,3},{3,1},... | collective-permute-start | bytes 98312 | tf_op jit(solution)/shard_map/ppermute | solution.py:181
  1.5 10.9 %collective-permute-start.9 = (bf16[128,128]{1,0:T(8,128)(2,1)S(1)}, bf16[128,128]{1,0:T(8,128)(2,1)S(1)}, u32[]{:S(2)}, u32[]{:S(2)}) collective-permute-start(bf16[128,128]{1,0:T(8,128)(2,1)S(1)} %get-tuple-element.42), channel_id=1, source_target_pairs={{0,4},{2,6},{4,0},{6,2},{8,12},{10,14},{12,8},{14,10},{1,5},{3,7},... | collective-permute-start | bytes 98312 | tf_op jit(solution)/shard_map/ppermute | solution.py:181
  4.1 8.4 %collective-permute-start.10 = (bf16[128,128]{1,0:T(8,128)(2,1)S(1)}, bf16[128,128]{1,0:T(8,128)(2,1)S(1)}, u32[]{:S(2)}, u32[]{:S(2)}) collective-permute-start(bf16[128,128]{1,0:T(8,128)(2,1)S(1)} %get-tuple-element.41), channel_id=1, source_target_pairs={{0,6},{2,4},{4,2},{6,0},{8,14},{10,12},{12,10},{14,8},{1,7},{3,5},... | collective-permute-start | bytes 98312 | tf_op jit(solution)/shard_map/ppermute | solution.py:181
  4.2 10.6 %collective-permute-start.11 = (bf16[128,128]{1,0:T(8,128)(2,1)S(1)}, bf16[128,128]{1,0:T(8,128)(2,1)S(1)}, u32[]{:S(2)}, u32[]{:S(2)}) collective-permute-start(bf16[128,128]{1,0:T(8,128)(2,1)S(1)} %get-tuple-element.40), channel_id=1, source_target_pairs={{0,8},{2,10},{4,12},{6,14},{8,0},{10,2},{12,4},{14,6},{1,9},{3,11}... | collective-permute-start | bytes 98312 | tf_op jit(solution)/shard_map/ppermute | solution.py:181
  6.9 7.8 %collective-permute-start.12 = (bf16[128,128]{1,0:T(8,128)(2,1)S(1)}, bf16[128,128]{1,0:T(8,128)(2,1)S(1)}, u32[]{:S(2)}, u32[]{:S(2)}) collective-permute-start(bf16[128,128]{1,0:T(8,128)(2,1)S(1)} %get-tuple-element.39), channel_id=1, source_target_pairs={{0,10},{2,8},{4,14},{6,12},{8,2},{10,0},{12,6},{14,4},{1,11},{3,9}... | collective-permute-start | bytes 98312 | tf_op jit(solution)/shard_map/ppermute | solution.py:181
  8.7 6.1 %collective-permute-start.13 = (bf16[128,128]{1,0:T(8,128)(2,1)S(1)}, bf16[128,128]{1,0:T(8,128)(2,1)S(1)}, u32[]{:S(2)}, u32[]{:S(2)}) collective-permute-start(bf16[128,128]{1,0:T(8,128)(2,1)S(1)} %get-tuple-element.38), channel_id=1, source_target_pairs={{0,12},{2,14},{4,8},{6,10},{8,4},{10,6},{12,0},{14,2},{1,13},{3,15... | collective-permute-start | bytes 98312 | tf_op jit(solution)/shard_map/ppermute | solution.py:181
  12.4 5.2 %collective-permute-start.14 = (bf16[128,128]{1,0:T(8,128)(2,1)S(1)}, bf16[128,128]{1,0:T(8,128)(2,1)S(1)}, u32[]{:S(2)}, u32[]{:S(2)}) collective-permute-start(bf16[128,128]{1,0:T(8,128)(2,1)S(1)} %get-tuple-element.37), channel_id=1, source_target_pairs={{0,14},{2,12},{4,10},{6,8},{8,6},{10,4},{12,2},{14,0},{1,15},{3,13... | collective-permute-start | bytes 98312 | tf_op jit(solution)/shard_map/ppermute | solution.py:181
  12.5 6.6 %collective-permute-start = (bf16[2048,128]{1,0:T(8,128)(2,1)}, bf16[2048,128]{1,0:T(8,128)(2,1)S(1)}, u32[]{:S(2)}, u32[]{:S(2)}) collective-permute-start(bf16[2048,128]{1,0:T(8,128)(2,1)} %x_ref.1), channel_id=1, source_target_pairs={{0,2},{2,4},{4,6},{6,8},{8,10},{10,12},{12,14},{1,3},{3,5},{5,7},{... | collective-permute-start | bytes 1572872 | tf_op jit(solution)/shard_map/ppermute | solution.py:183
  17.6 19.8 %collective-permute-start.15 = (bf16[8,128,128]{2,1,0:T(8,128)(2,1)S(1)}, bf16[8,128,128]{2,1,0:T(8,128)(2,1)S(1)}, u32[]{:S(2)}, u32[]{:S(2)}) collective-permute-start(bf16[8,128,128]{2,1,0:T(8,128)(2,1)S(1)} %bitcast_dynamic-update-slice_fusion.mine_ref), channel_id=1, source_target_pairs={{0,16},{16,0},{1,17},{17,1},{2,18},{18,2},{3,19},{19,3},{4,20},{20... | collective-permute-start | bytes 786440 | tf_op jit(solution)/shard_map/ppermute | solution.py:192
  19.1 1.0 %copy-start.2 = (bf16[2048,128]{1,0:T(8,128)(2,1)S(1)}, bf16[2048,128]{1,0:T(8,128)(2,1)}, u32[]{:S(2)}) copy-start(bf16[2048,128]{1,0:T(8,128)(2,1)} %x_ref.1) | copy-start | bytes 1572868
  20.2 1.0 %copy-start.3 = (bf16[2048,128]{1,0:T(8,128)(2,1)S(1)}, bf16[2048,128]{1,0:T(8,128)(2,1)}, u32[]{:S(2)}) copy-start(bf16[2048,128]{1,0:T(8,128)(2,1)} %gate_ref.1) | copy-start | bytes 1572868
  21.2 1.0 %copy-start.4 = (bf16[2048,128]{1,0:T(8,128)(2,1)S(1)}, bf16[2048,128]{1,0:T(8,128)(2,1)}, u32[]{:S(2)}) copy-start(bf16[2048,128]{1,0:T(8,128)(2,1)} %taps_ref.1) | copy-start | bytes 1572868
  22.3 0.9 %copy-start.5 = (bf16[256,256]{1,0:T(8,128)(2,1)S(1)}, bf16[256,256]{1,0:T(8,128)(2,1)}, u32[]{:S(2)}) copy-start(bf16[256,256]{1,0:T(8,128)(2,1)} %constant.43.clone.hi_ref.refs_9_) | copy-start | bytes 393220
  23.2 0.9 %copy-start.7 = (bf16[256,256]{1,0:T(8,128)(2,1)S(1)}, bf16[256,256]{1,0:T(8,128)(2,1)}, u32[]{:S(2)}) copy-start(bf16[256,256]{1,0:T(8,128)(2,1)} %constant.44.clone.lo_ref.refs_10_) | copy-start | bytes 393220
  24.1 0.9 %copy-start.9 = (bf16[256,256]{1,0:T(8,128)(2,1)S(1)}, bf16[256,256]{1,0:T(8,128)(2,1)}, u32[]{:S(2)}) copy-start(bf16[256,256]{1,0:T(8,128)(2,1)} %constant.46.clone.both_ref.refs_11_) | copy-start | bytes 393220
  25.0 0.9 %copy-start.11 = (bf16[256,256]{1,0:T(8,128)(2,1)S(1)}, bf16[256,256]{1,0:T(8,128)(2,1)}, u32[]{:S(2)}) copy-start(bf16[256,256]{1,0:T(8,128)(2,1)} %constant.45.clone.top_ref) | copy-start | bytes 393220
  25.9 15.4 %copy-start.6 = (bf16[256,256]{1,0:T(8,128)(2,1)S(1)}, bf16[256,256]{1,0:T(8,128)(2,1)}, u32[]{:S(2)}) copy-start(bf16[256,256]{1,0:T(8,128)(2,1)} %constant.43.clone.hi_ref.refs_9_) | copy-start | bytes 393220
  25.9 15.4 %copy-start.8 = (bf16[256,256]{1,0:T(8,128)(2,1)S(1)}, bf16[256,256]{1,0:T(8,128)(2,1)}, u32[]{:S(2)}) copy-start(bf16[256,256]{1,0:T(8,128)(2,1)} %constant.44.clone.lo_ref.refs_10_) | copy-start | bytes 393220
  25.9 15.4 %copy-start.10 = (bf16[256,256]{1,0:T(8,128)(2,1)S(1)}, bf16[256,256]{1,0:T(8,128)(2,1)}, u32[]{:S(2)}) copy-start(bf16[256,256]{1,0:T(8,128)(2,1)} %constant.46.clone.both_ref.refs_11_) | copy-start | bytes 393220
  25.9 15.4 %copy-start.12 = (bf16[256,256]{1,0:T(8,128)(2,1)S(1)}, bf16[256,256]{1,0:T(8,128)(2,1)}, u32[]{:S(2)}) copy-start(bf16[256,256]{1,0:T(8,128)(2,1)} %constant.45.clone.top_ref) | copy-start | bytes 393220
  28.9 8.5 %collective-permute-start.1 = (bf16[256,128]{1,0:T(8,128)(2,1)S(1)}, bf16[256,128]{1,0:T(8,128)(2,1)S(1)}, u32[]{:S(2)}, u32[]{:S(2)}) collective-permute-start(bf16[256,128]{1,0:T(8,128)(2,1)S(1)} %get-tuple-element.22), channel_id=1, source_target_pairs={{0,2},{2,0},{4,6},{6,4},{8,10},{10,8},{12,14},{14,12},{1,3},{3,1},... | collective-permute-start | bytes 196616 | tf_op jit(solution)/shard_map/ppermute | solution.py:181
  31.0 10.2 %collective-permute-start.2 = (bf16[256,128]{1,0:T(8,128)(2,1)S(1)}, bf16[256,128]{1,0:T(8,128)(2,1)S(1)}, u32[]{:S(2)}, u32[]{:S(2)}) collective-permute-start(bf16[256,128]{1,0:T(8,128)(2,1)S(1)} %get-tuple-element.23), channel_id=1, source_target_pairs={{0,4},{2,6},{4,0},{6,2},{8,12},{10,14},{12,8},{14,10},{1,5},{3,7},... | collective-permute-start | bytes 196616 | tf_op jit(solution)/shard_map/ppermute | solution.py:181
  33.3 11.1 %collective-permute-start.3 = (bf16[256,128]{1,0:T(8,128)(2,1)S(1)}, bf16[256,128]{1,0:T(8,128)(2,1)S(1)}, u32[]{:S(2)}, u32[]{:S(2)}) collective-permute-start(bf16[256,128]{1,0:T(8,128)(2,1)S(1)} %get-tuple-element.24), channel_id=1, source_target_pairs={{0,6},{2,4},{4,2},{6,0},{8,14},{10,12},{12,10},{14,8},{1,7},{3,5},... | collective-permute-start | bytes 196616 | tf_op jit(solution)/shard_map/ppermute | solution.py:181
  33.4 11.0 %collective-permute-start.4 = (bf16[256,128]{1,0:T(8,128)(2,1)S(1)}, bf16[256,128]{1,0:T(8,128)(2,1)S(1)}, u32[]{:S(2)}, u32[]{:S(2)}) collective-permute-start(bf16[256,128]{1,0:T(8,128)(2,1)S(1)} %get-tuple-element.25), channel_id=1, source_target_pairs={{0,8},{2,10},{4,12},{6,14},{8,0},{10,2},{12,4},{14,6},{1,9},{3,11}... | collective-permute-start | bytes 196616 | tf_op jit(solution)/shard_map/ppermute | solution.py:181
  37.4 10.6 %collective-permute-start.5 = (bf16[256,128]{1,0:T(8,128)(2,1)S(1)}, bf16[256,128]{1,0:T(8,128)(2,1)S(1)}, u32[]{:S(2)}, u32[]{:S(2)}) collective-permute-start(bf16[256,128]{1,0:T(8,128)(2,1)S(1)} %get-tuple-element.26), channel_id=1, source_target_pairs={{0,10},{2,8},{4,14},{6,12},{8,2},{10,0},{12,6},{14,4},{1,11},{3,9}... | collective-permute-start | bytes 196616 | tf_op jit(solution)/shard_map/ppermute | solution.py:181
  37.4 10.6 %collective-permute-start.6 = (bf16[256,128]{1,0:T(8,128)(2,1)S(1)}, bf16[256,128]{1,0:T(8,128)(2,1)S(1)}, u32[]{:S(2)}, u32[]{:S(2)}) collective-permute-start(bf16[256,128]{1,0:T(8,128)(2,1)S(1)} %get-tuple-element.27), channel_id=1, source_target_pairs={{0,12},{2,14},{4,8},{6,10},{8,4},{10,6},{12,0},{14,2},{1,13},{3,15... | collective-permute-start | bytes 196616 | tf_op jit(solution)/shard_map/ppermute | solution.py:181
  41.1 6.9 %collective-permute-start.7 = (bf16[256,128]{1,0:T(8,128)(2,1)S(1)}, bf16[256,128]{1,0:T(8,128)(2,1)S(1)}, u32[]{:S(2)}, u32[]{:S(2)}) collective-permute-start(bf16[256,128]{1,0:T(8,128)(2,1)S(1)} %get-tuple-element.28), channel_id=1, source_target_pairs={{0,14},{2,12},{4,10},{6,8},{8,6},{10,4},{12,2},{14,0},{1,15},{3,13... | collective-permute-start | bytes 196616 | tf_op jit(solution)/shard_map/ppermute | solution.py:181
  48.0 19.7 %copy-start.1 = (bf16[2048,128]{1,0:T(8,128)(2,1)S(1)}, bf16[2048,128]{1,0:T(8,128)(2,1)}, u32[]{:S(2)}) copy-start(bf16[2048,128]{1,0:T(8,128)(2,1)} %refs_8_.1) | copy-start | bytes 1572868
  51.5 6.1 %collective-permute-start.16 = (bf16[256,128]{1,0:T(8,128)(2,1)S(1)}, bf16[256,128]{1,0:T(8,128)(2,1)S(1)}, u32[]{:S(2)}, u32[]{:S(2)}) collective-permute-start(bf16[256,128]{1,0:T(8,128)(2,1)S(1)} %get-tuple-element.30), channel_id=1, source_target_pairs={{0,2},{2,0},{4,6},{6,4},{8,10},{10,8},{12,14},{14,12},{1,3},{3,1},... | collective-permute-start | bytes 196616 | tf_op jit(solution)/shard_map/ppermute | solution.py:181
  51.6 8.0 %collective-permute-start.17 = (bf16[256,128]{1,0:T(8,128)(2,1)S(1)}, bf16[256,128]{1,0:T(8,128)(2,1)S(1)}, u32[]{:S(2)}, u32[]{:S(2)}) collective-permute-start(bf16[256,128]{1,0:T(8,128)(2,1)S(1)} %get-tuple-element.31), channel_id=1, source_target_pairs={{0,4},{2,6},{4,0},{6,2},{8,12},{10,14},{12,8},{14,10},{1,5},{3,7},... | collective-permute-start | bytes 196616 | tf_op jit(solution)/shard_map/ppermute | solution.py:181
  55.0 6.2 %collective-permute-start.18 = (bf16[256,128]{1,0:T(8,128)(2,1)S(1)}, bf16[256,128]{1,0:T(8,128)(2,1)S(1)}, u32[]{:S(2)}, u32[]{:S(2)}) collective-permute-start(bf16[256,128]{1,0:T(8,128)(2,1)S(1)} %get-tuple-element.32), channel_id=1, source_target_pairs={{0,6},{2,4},{4,2},{6,0},{8,14},{10,12},{12,10},{14,8},{1,7},{3,5},... | collective-permute-start | bytes 196616 | tf_op jit(solution)/shard_map/ppermute | solution.py:181
  55.0 6.2 %collective-permute-start.19 = (bf16[256,128]{1,0:T(8,128)(2,1)S(1)}, bf16[256,128]{1,0:T(8,128)(2,1)S(1)}, u32[]{:S(2)}, u32[]{:S(2)}) collective-permute-start(bf16[256,128]{1,0:T(8,128)(2,1)S(1)} %get-tuple-element.33), channel_id=1, source_target_pairs={{0,8},{2,10},{4,12},{6,14},{8,0},{10,2},{12,4},{14,6},{1,9},{3,11}... | collective-permute-start | bytes 196616 | tf_op jit(solution)/shard_map/ppermute | solution.py:181
  57.5 10.2 %collective-permute-start.20 = (bf16[256,128]{1,0:T(8,128)(2,1)S(1)}, bf16[256,128]{1,0:T(8,128)(2,1)S(1)}, u32[]{:S(2)}, u32[]{:S(2)}) collective-permute-start(bf16[256,128]{1,0:T(8,128)(2,1)S(1)} %get-tuple-element.34), channel_id=1, source_target_pairs={{0,10},{2,8},{4,14},{6,12},{8,2},{10,0},{12,6},{14,4},{1,11},{3,9}... | collective-permute-start | bytes 196616 | tf_op jit(solution)/shard_map/ppermute | solution.py:181
  57.5 10.2 %collective-permute-start.21 = (bf16[256,128]{1,0:T(8,128)(2,1)S(1)}, bf16[256,128]{1,0:T(8,128)(2,1)S(1)}, u32[]{:S(2)}, u32[]{:S(2)}) collective-permute-start(bf16[256,128]{1,0:T(8,128)(2,1)S(1)} %get-tuple-element.35), channel_id=1, source_target_pairs={{0,12},{2,14},{4,8},{6,10},{8,4},{10,6},{12,0},{14,2},{1,13},{3,15... | collective-permute-start | bytes 196616 | tf_op jit(solution)/shard_map/ppermute | solution.py:181
  59.7 8.1 %collective-permute-start.22 = (bf16[256,128]{1,0:T(8,128)(2,1)S(1)}, bf16[256,128]{1,0:T(8,128)(2,1)S(1)}, u32[]{:S(2)}, u32[]{:S(2)}) collective-permute-start(bf16[256,128]{1,0:T(8,128)(2,1)S(1)} %get-tuple-element.36), channel_id=1, source_target_pairs={{0,14},{2,12},{4,10},{6,8},{8,6},{10,4},{12,2},{14,0},{1,15},{3,13... | collective-permute-start | bytes 196616 | tf_op jit(solution)/shard_map/ppermute | solution.py:181

commit v2 on v1

v2 whole, which is shorter than its diff:
```python
import functools
import math

import jax
import jax.numpy as jnp
import numpy as np
from jax import lax
from jax.experimental import pallas as pl
from jax.experimental.pallas import tpu as pltpu
from jax.sharding import PartitionSpec as P


AXES = ("tok", "sec")
F32 = jnp.float32
BF16 = jnp.bfloat16


def split_const(matrix):
    hi = matrix.astype(np.float32).astype(jnp.bfloat16)
    lo = (matrix - hi.astype(np.float64)).astype(np.float32).astype(jnp.bfloat16)
    return hi, lo


def tables(block):
    length = 2 * block
    sample = np.arange(length)[:, None]
    freq = np.arange(block)[None, :]
    turns = (sample * (2 * freq + 1)) % (2 * length)
    angle = turns * (math.pi / length)
    forward = np.concatenate([np.cos(angle), -np.sin(angle)], axis=1)
    hi, lo = split_const(forward)
    top = np.concatenate([hi[:block], lo[:block]], axis=0)
    back = forward[block:].T / block
    back_hi, back_lo = split_const(back)
    both = np.concatenate([back_hi, back_lo], axis=1)
    return jnp.asarray(np.concatenate([hi, lo, top, both], axis=0))


def parts_of(table_ref):
    n = table_ref.shape[1]
    return tuple(table_ref[i * n : (i + 1) * n, :] for i in range(4))


def mm(left, right):
    return jnp.dot(left, right, preferred_element_type=F32)


def window_spectrum(before, here, hi, lo):
    window = jnp.concatenate([before, here], axis=1)
    return mm(window, hi) + mm(window, lo)


def block_spectrum(rows, top):
    return mm(jnp.concatenate([rows, rows], axis=1), top)


def two_parts(value):
    hi = value.astype(BF16)
    return hi, (value - hi.astype(F32)).astype(BF16)


def times(left, right):
    n = left.shape[-1] // 2
    lr, li, rr, ri = left[:, :n], left[:, n:], right[:, :n], right[:, n:]
    return jnp.concatenate([lr * rr - li * ri, lr * ri + li * rr], axis=1)


def valid_part(spectrum, both):
    n = both.shape[1] // 2
    hi, lo = two_parts(spectrum)
    wide = mm(hi, both)
    return wide[:, :n] + wide[:, n:] + mm(lo, both[:, :n])


def rows_at(index, rows):
    return pl.ds(pl.multiple_of(index * rows, rows), rows)


def first_kernel(which, me_ref, halo_ref, table_ref, *refs):
    count = len(which)
    outs = refs[3 * count :]
    rows = outs[0].shape[0]
    me = me_ref[0]
    hi, lo, top, both = parts_of(table_ref)
    for i, k in enumerate(which):
        x_ref, gate_ref, taps_ref = refs[3 * i : 3 * i + 3]
        spectrum = window_spectrum(halo_ref[rows_at(me ^ k, rows), :], x_ref[...], hi, lo)
        taps = block_spectrum(taps_ref[...], top)
        conv = valid_part(times(spectrum, taps), both)
        outs[i][...] = (conv * gate_ref[...].astype(F32)).astype(BF16)


def filter_kernel(shards, me_ref, mine_ref, other_ref, taps_ref, skip_ref, table_ref, out_ref, lags, taps_hat):
    half = mine_ref.shape[1]
    me, group = me_ref[0], me_ref[1]
    hi, lo, top, both = parts_of(table_ref)
    lags[0] = jnp.zeros(lags.shape[1:], BF16)
    for k in range(shards):
        lags[(me ^ k) + 1, rows_at(group, half), :] = mine_ref[k]
        lags[(me ^ k) + 1, rows_at(1 - group, half), :] = other_ref[k]
    taps_hat[...] = block_spectrum(taps_ref[...], top)
    for m in range(shards):
        spectrum = window_spectrum(lags[m], lags[m + 1], hi, lo)
        joined = valid_part(times(spectrum, taps_hat[...]), both)
        part_hi, part_lo = two_parts(joined)
        n = part_hi.shape[1]
        result = block_spectrum(part_hi, top) + mm(part_lo, top[:n])
        if m == 0:
            result = result + skip_ref[...] * taps_hat[...]
        out_ref[m] = result


def lead_kernel(shards, lead, me_ref, *refs):
    pieces = refs[:shards]
    filt_ref, table_ref, out_ref, spectra, signal, total = refs[shards:]
    rows, block = pieces[0].shape
    me = me_ref[0]
    hi, lo, _, both = parts_of(table_ref)
    signal[0] = jnp.zeros((rows, block), BF16)
    for k in range(shards):
        signal[(me ^ k) + 1] = pieces[k][...]
    for j in range(shards):
        spectra[j] = window_spectrum(signal[j], signal[j + 1], hi, lo)
    j = me ^ lead
    tile = min(64, rows)

    def row_tile(i, carry):
        at = pl.ds(pl.multiple_of(i * tile, tile), tile)

        def term(m, sums):
            fr, fi = filt_ref[m, at, :block], filt_ref[m, at, block:]
            sr, si = spectra[j - m, at, :block], spectra[j - m, at, block:]
            return sums[0] + (fr * sr - fi * si), sums[1] + (fr * si + fi * sr)

        zero = jnp.zeros((tile, block), F32)
        re, im = lax.fori_loop(0, j + 1, term, (zero, zero))
        total[at, :block] = re
        total[at, block:] = im
        return carry

    lax.fori_loop(0, rows // tile, row_tile, 0)
    out_ref[...] = valid_part(total[...], both).astype(BF16)


def long_kernel(shards, which, me_ref, filt_ref, spectra, table_ref, *refs):
    outs, sums = refs[:-1], refs[-1]
    rows, block = outs[0].shape
    me = me_ref[0]
    both = parts_of(table_ref)[3]
    tile = 8

    def body(i, carry):
        at = pl.ds(pl.multiple_of(i * tile, tile), tile)
        fr = [filt_ref[m, at, :block] for m in range(shards)]
        fi = [filt_ref[m, at, block:] for m in range(shards)]
        sr = [spectra[m, at, :block] for m in range(shards)]
        si = [spectra[m, at, block:] for m in range(shards)]
        for j in range(shards):
            re = fr[0] * sr[j] - fi[0] * si[j]
            im = fr[0] * si[j] + fi[0] * sr[j]
            for m in range(1, j + 1):
                re = re + (fr[m] * sr[j - m] - fi[m] * si[j - m])
                im = im + (fr[m] * si[j - m] + fi[m] * sr[j - m])
            sums[j, at, :block] = re
            sums[j, at, block:] = im
        return carry

    lax.fori_loop(0, rows // tile, body, 0)
    for k, out_ref in zip(which, outs):
        out_ref[...] = valid_part(sums[me ^ k], both).astype(BF16)


def last_kernel(order, me_ref, *refs):
    count = len(order)
    pieces, gates = refs[:count], refs[count : 2 * count]
    out_ref, made, sems = refs[2 * count :]
    rows = pieces[0].shape[0]
    me = me_ref[0]
    copies = []
    for i, k in enumerate(order):
        at = rows_at(me ^ k, rows)
        made[i] = (pieces[i][...].astype(F32) * gates[i][...].astype(F32)).astype(BF16)
        copies.append(pltpu.make_async_copy(made.at[i], out_ref.at[at, :], sems.at[i]))
        copies[-1].start()
    for copy in copies:
        copy.wait()


VMEM = pl.BlockSpec(memory_space=pltpu.VMEM)
HBM = pl.BlockSpec(memory_space=pltpu.HBM)


def size_of(arrays):
    return sum(math.prod(a.shape) * a.dtype.itemsize for a in arrays)


def call(kernel, inputs, out_shape, scratch=(), flops=0, in_space=VMEM, out_space=VMEM, limit=28 * 2**20):
    moved = size_of(inputs)
    many = isinstance(out_shape, (list, tuple))
    return pl.pallas_call(
        kernel,
        out_shape=out_shape,
        in_specs=[pl.BlockSpec(memory_space=pltpu.SMEM)] + [in_space] * (len(inputs) - 1),
        out_specs=[out_space] * len(out_shape) if many else out_space,
        scratch_shapes=list(scratch),
        compiler_params=pltpu.CompilerParams(vmem_limit_bytes=limit),
        cost_estimate=pl.CostEstimate(flops=flops, bytes_accessed=moved, transcendentals=0),
    )(*inputs)


def far_first(shards):
    order = []
    step = shards // 2
    while step:
        order += list(range(step, 2 * step))
        step //= 2
    return order


def stages(features, gate_one, taps_one, long_filter, skip_gain, taps_two, gate_two):
    shards = lax.axis_size(AXES)
    groups = lax.axis_size("grp")
    assert shards & (shards - 1) == 0 and groups == 2
    channels, block = features.shape
    assert taps_one.shape[1] == block and taps_two.shape[1] == block
    narrow = channels // shards
    half = narrow // groups
    me = lax.axis_index(AXES)
    place = jnp.stack([me, lax.axis_index("grp")]).astype(jnp.int32)
    flops = 2 * channels * 256 * 256
    order = far_first(shards)
    lead = order[0]
    rest = order[1:] + [0]

    def swapped(piece, k):
        if k == 0:
            return piece
        return lax.ppermute(piece, AXES, [(i, i ^ k) for i in range(shards)])

    halo = lax.ppermute(features, AXES, [(i, i + 1) for i in range(shards - 1)])

    def rows_for(array, k):
        return lax.dynamic_slice_in_dim(array, (me ^ k) * narrow, narrow)

    table = tables(block)
    by_owner = long_filter.reshape(shards, groups, half, block)
    group = lax.axis_index("grp")
    lags = [
        lax.dynamic_slice(by_owner, (me ^ k, group, 0, 0), (1, 1, half, block)).reshape(half, block)
        for k in range(shards)
    ]
    mine = jnp.stack([swapped(lags[k], k) for k in range(shards)])
    other = lax.ppermute(mine, "grp", [(0, 1), (1, 0)])

    piece = jax.ShapeDtypeStruct((narrow, block), BF16)

    def operands(which):
        cuts = []
        for k in which:
            cuts += [rows_for(features, k), rows_for(gate_one, k), rows_for(taps_one, k)]
        return (place, halo, table, *cuts)

    (front,) = call(functools.partial(first_kernel, [lead]), operands([lead]), [piece], flops=flops)
    others = call(functools.partial(first_kernel, rest), operands(rest), [piece] * len(rest), flops=6 * flops)
    mixed = {k: swapped(p, k) for k, p in zip([lead] + rest, [front] + list(others))}

    skip_late, taps_late, gate_late, _ = lax.optimization_barrier((skip_gain, taps_two, gate_two, others[0]))
    skip_local = rows_for(skip_late, 0)[:, None]
    taps_local = rows_for(taps_late, 0)
    spectrum = jax.ShapeDtypeStruct((shards, narrow, 2 * block), F32)
    joined = call(
        functools.partial(filter_kernel, shards),
        (place, mine, other, taps_local, skip_local, table),
        spectrum,
        scratch=[
            pltpu.VMEM((shards + 1, narrow, block), BF16),
            pltpu.VMEM((narrow, 2 * block), F32),
        ],
        flops=6 * flops,
    )
    front, spectra = call(
        functools.partial(lead_kernel, shards, lead),
        (place, *[mixed[k] for k in range(shards)], joined, table),
        [piece, spectrum],
        scratch=[
            pltpu.VMEM((shards + 1, narrow, block), BF16),
            pltpu.VMEM((narrow, 2 * block), F32),
        ],
        flops=3 * flops,
    )
    others = call(
        functools.partial(long_kernel, shards, rest),
        (place, joined, spectra, table),
        [piece] * len(rest),
        scratch=[pltpu.VMEM((shards, narrow, 2 * block), F32)],
        flops=3 * flops,
    )
    result = {k: swapped(p, k) for k, p in zip([lead] + rest, [front] + list(others))}
    ready = [0] + order[::-1]
    return call(
        functools.partial(last_kernel, ready),
        (place, *[result[k] for k in ready], *[rows_for(gate_late, k) for k in ready]),
        jax.ShapeDtypeStruct((channels, block), BF16),
        scratch=[
            pltpu.VMEM((shards, narrow, block), BF16),
            pltpu.SemaphoreType.DMA((shards,)),
        ],
        flops=channels * block,
        out_space=HBM,
    )


def solution(mesh):
    in_specs = (
        P("ch", ("grp", "tok", "sec")),
        P("ch", ("grp", "tok", "sec")),
        P("ch", None),
        P("ch", ("tok", "sec")),
        P("ch"),
        P("ch", None),
        P("ch", ("grp", "tok", "sec")),
    )
    out_specs = P("ch", ("grp", "tok", "sec"))
    return jax.shard_map(stages, mesh=mesh, in_specs=in_specs, out_specs=out_specs, check_vma=False)
```

time: 70.3 us -> 63.6 us (0.905)
  local copies, waits for them, and re-layouts: 9.42 us -> 3.94 us
  starting transfers between devices: 35.6 us -> 32.2 us
  Pallas kernels: 11 us -> 12.6 us
  waiting for transfers between devices: 13 us -> 14.2 us
    unnamed x33 -> x17, local copies, waits for them, and re-layouts: 7.58 us -> 0.84 us
    ppermute x21, starting transfers between devices: 31.9 us -> 28.1 us  [swapped(): return lax.ppermute(piece, AXES, [(i, i ^ k) for i in range(shards)])]
    pallas_call x4 -> x6, Pallas kernels: 11 us -> 12.6 us  [call(): pl.pallas_call(kernel, out_shape=out_shape, in_specs=[pl.BlockSpec(memory...]
    dynamic_slice x2 -> x5, local copies, waits for them, and re-layouts: 0.76 us -> 2.01 us  [rows_for(): return lax.dynamic_slice_in_dim(array, (me ^ k) * narrow, narrow)]
    ppermute x21, waiting for transfers between devices: 13 us -> 14.2 us  [swapped(): return lax.ppermute(piece, AXES, [(i, i ^ k) for i in range(shards)])]
  transfers between devices with their start and end apart: 23 -> 23, of which waited for: 3 -> 8; matrix products, arithmetic and copies ran while one was open for 3% -> 6% of each run, Pallas kernels for 9% -> 11%
where the time goes in v2:
time: 63.6 us; the launch traced here: 63.3 us
  starting transfers between devices  32.2 us (51%)
  waiting for transfers between devices  14.2 us (22%)
  Pallas kernels  12.6 us (20%)
  local copies, waits for them, and re-layouts  3.94 us (6%)
    ppermute x21, starting transfers between devices, swapped(): return lax.ppermute(piece, AXES, [(i, i ^ k) for i in range(shards)])  28.1 us
    ppermute x21, waiting for transfers between devices, swapped(): return lax.ppermute(piece, AXES, [(i, i ^ k) for i in range(shards)])  14.2 us
    pallas_call x6, Pallas kernels, call(): pl.pallas_call(kernel, out_shape=out_shape, in_specs=[pl.BlockSpec(memory...  12.6 us
    ppermute x1, starting transfers between devices, stages(): halo = lax.ppermute(features, AXES, [(i, i + 1) for i in range(shards - 1)])  2.57 us
    dynamic_slice x5, local copies, waits for them, and re-layouts, rows_for(): return lax.dynamic_slice_in_dim(array, (me ^ k) * narrow, narrow)  2.01 us
    ppermute x1, starting transfers between devices, stages(): other = lax.ppermute(mine, 'grp', [(0, 1), (1, 0)])  1.52 us
  transfers between devices with their start and end apart: 23, of which 8 were waited for; matrix products, arithmetic and copies ran while one was open for 6% of the time, Pallas kernels for 11%

profile of v2, /device:TPU:0, one launch (start us, length us, event | category | flops | bytes accessed | tf_op | source)
XLA Modules:
  0.0 63.3 jit_solution(3447491175059381675)
XLA Ops:
  0.0 0.0 copy-start
  0.0 2.6 %collective-permute-start.8 = (bf16[2048,128]{1,0:T(8,128)(2,1)}, bf16[2048,128]{1,0:T(8,128)(2,1)S(1)}, u32[]{:S(2)}, u32[]{:S(2)}) collective-permute-start(bf16[2048,128]{1,0:T(8,128)(2,1)} %param.8), channel_id=1, source_target_pairs={{0,2},{2,4},{4,6},{6,8},{8,10},{10,12},{12,14},{1,3},{3,5},{5,7},{... | collective-permute-start | bytes 1572872 | tf_op jit(solution)/shard_map/ppermute | solution.py:240
  2.6 0.0 copy-start.1
  2.7 0.9 %dynamic-slice_bitcast_fusion = (bf16[128,128]{1,0:T(8,128)(2,1)S(1)}, bf16[128,128]{1,0:T(8,128)(2,1)S(1)}, bf16[128,128]{1,0:T(8,128)(2,1)S(1)}, bf16[128,128]...) fusion(bf16[8,2,128,128]{3,2,1,0:T(8,128)(2,1)} %bitcast.34, ...), kind=kLoop, calls=%fused_computation.8 | loop fusion | bytes 458784 | tf_op jit(solution)/shard_map/reshape | solution.py:249
  3.6 2.7 %collective-permute-start = (bf16[128,128]{1,0:T(8,128)(2,1)S(1)}, bf16[128,128]{1,0:T(8,128)(2,1)S(1)}, u32[]{:S(2)}, u32[]{:S(2)}) collective-permute-start(bf16[128,128]{1,0:T(8,128)(2,1)S(1)} %get-tuple-element.81), channel_id=1, source_target_pairs={{0,2},{2,0},{4,6},{6,4},{8,10},{10,8},{12,14},{14,12},{1,3},{3,1},... | collective-permute-start | bytes 98312 | tf_op jit(solution)/shard_map/ppermute | solution.py:238
  6.3 1.6 %collective-permute-start.1 = (bf16[128,128]{1,0:T(8,128)(2,1)S(1)}, bf16[128,128]{1,0:T(8,128)(2,1)S(1)}, u32[]{:S(2)}, u32[]{:S(2)}) collective-permute-start(bf16[128,128]{1,0:T(8,128)(2,1)S(1)} %get-tuple-element.80), channel_id=1, source_target_pairs={{0,4},{2,6},{4,0},{6,2},{8,12},{10,14},{12,8},{14,10},{1,5},{3,7},... | collective-permute-start | bytes 98312 | tf_op jit(solution)/shard_map/ppermute | solution.py:238
  7.9 0.0 collective-permute-start.2
  7.9 2.4 %collective-permute-start.3 = (bf16[128,128]{1,0:T(8,128)(2,1)S(1)}, bf16[128,128]{1,0:T(8,128)(2,1)S(1)}, u32[]{:S(2)}, u32[]{:S(2)}) collective-permute-start(bf16[128,128]{1,0:T(8,128)(2,1)S(1)} %get-tuple-element.78), channel_id=1, source_target_pairs={{0,8},{2,10},{4,12},{6,14},{8,0},{10,2},{12,4},{14,6},{1,9},{3,11}... | collective-permute-start | bytes 98312 | tf_op jit(solution)/shard_map/ppermute | solution.py:238
  10.3 0.8 %bitcast_dynamic-update-slice_fusion.7 = bf16[8,128,128]{2,1,0:T(8,128)(2,1)S(1)} fusion(bf16[8,2,128,128]{3,2,1,0:T(8,128)(2,1)} %bitcast.35, s32[]{:T(128)S(6)} %select_n.34, s32[]{:T(128)S(6)} %select_n.35), kind=kLoop, calls=%fused_computation.7 | loop fusion | bytes 65544
  11.1 1.1 %constant_dynamic-slice_fusion.10 = (bf16[256,128]{1,0:T(8,128)(2,1)S(1)}, bf16[256,128]{1,0:T(8,128)(2,1)S(1)}, bf16[256,128]{1,0:T(8,128)(2,1)S(1)}, bf16[256,...) fusion(bf16[2048,128]{1,0:T(8,128)(2,1)} %param.8, ...), kind=kLoop, calls=%fused_computation.25 | loop fusion | bytes 1048608 | tf_op jit(solution)/shard_map/dynamic_slice | solution.py:243
  12.2 0.0 copy-done.3
  12.2 0.1 constant_dynamic-slice_fusion.8
  12.3 0.1 pad_add_fusion.me_ref
  12.4 0.0 collective-permute-done
  12.4 0.4 collective-permute-start.4
  12.8 0.0 collective-permute-done.1
  12.8 2.1 %collective-permute-start.5 = (bf16[128,128]{1,0:T(8,128)(2,1)S(1)}, bf16[128,128]{1,0:T(8,128)(2,1)S(1)}, u32[]{:S(2)}, u32[]{:S(2)}) collective-permute-start(bf16[128,128]{1,0:T(8,128)(2,1)S(1)} %get-tuple-element.76), channel_id=1, source_target_pairs={{0,12},{2,14},{4,8},{6,10},{8,4},{10,6},{12,0},{14,2},{1,13},{3,15... | collective-permute-start | bytes 98312 | tf_op jit(solution)/shard_map/ppermute | solution.py:238
  14.9 0.0 collective-permute-done.2
  14.9 2.3 %collective-permute-start.6 = (bf16[128,128]{1,0:T(8,128)(2,1)S(1)}, bf16[128,128]{1,0:T(8,128)(2,1)S(1)}, u32[]{:S(2)}, u32[]{:S(2)}) collective-permute-start(bf16[128,128]{1,0:T(8,128)(2,1)S(1)} %get-tuple-element.75), channel_id=1, source_target_pairs={{0,14},{2,12},{4,10},{6,8},{8,6},{10,4},{12,2},{14,0},{1,15},{3,13... | collective-permute-start | bytes 98312 | tf_op jit(solution)/shard_map/ppermute | solution.py:238
  17.2 0.0 collective-permute-done.3
  17.2 0.4 collective-permute-done.4
  17.6 1.3 %collective-permute-done.5 = bf16[128,128]{1,0:T(8,128)(2,1)S(1)} collective-permute-done((bf16[128,128]{1,0:T(8,128)(2,1)S(1)}, bf16[128,128]{1,0:T(8,128)(2,1)S(1)}, u32[]{:S(2)}, u32[]{:S(2)}) %collective-permute-start.5) | collective-permute-done | bytes 32800 | tf_op jit(solution)/shard_map/ppermute | solution.py:238
  18.9 1.3 %collective-permute-done.6 = bf16[128,128]{1,0:T(8,128)(2,1)S(1)} collective-permute-done((bf16[128,128]{1,0:T(8,128)(2,1)S(1)}, bf16[128,128]{1,0:T(8,128)(2,1)S(1)}, u32[]{:S(2)}, u32[]{:S(2)}) %collective-permute-start.6) | collective-permute-done | bytes 32800 | tf_op jit(solution)/shard_map/ppermute | solution.py:238
  20.2 1.5 %collective-permute-start.7 = (bf16[8,128,128]{2,1,0:T(8,128)(2,1)S(1)}, bf16[8,128,128]{2,1,0:T(8,128)(2,1)S(1)}, u32[]{:S(2)}, u32[]{:S(2)}) collective-permute-start(bf16[8,128,128]{2,1,0:T(8,128)(2,1)S(1)} %bitcast_dynamic-update-slice_fusion.mine_ref), channel_id=1, source_target_pairs={{0,16},{16,0},{1,17},{17,1},{2,18},{18,2},{3,19},{19,3},{4,20},{20... | collective-permute-start | bytes 786440 | tf_op jit(solution)/shard_map/ppermute | solution.py:253
  21.7 0.0 collective-permute-done.8.halo_ref
  21.7 2.7 %shard_map.82 = (bf16[256,128]{1,0:T(8,128)(2,1)S(1)}, bf16[256,128]{1,0:T(8,128)(2,1)S(1)}, bf16[256,128]{1,0:T(8,128)(2,1)S(1)}, bf16[256,128]{1,0:T(8,128)(2,...) custom-call(s32[2]{0:T(128)S(1)} %pad_add_fusion.me_ref, ...), custom_call_target="tpu_custom_call" | custom-call | flops 1610612736 | bytes 2424840 | tf_op jit(solution)/shard_map/pallas_call | solution.py:200
  24.4 0.1 collective-permute-start.13
  24.5 2.8 %collective-permute-start.10 = (bf16[256,128]{1,0:T(8,128)(2,1)S(1)}, bf16[256,128]{1,0:T(8,128)(2,1)S(1)}, u32[]{:S(2)}, u32[]{:S(2)}) collective-permute-start(bf16[256,128]{1,0:T(8,128)(2,1)S(1)} %get-tuple-element.29), channel_id=1, source_target_pairs={{0,4},{2,6},{4,0},{6,2},{8,12},{10,14},{12,8},{14,10},{1,5},{3,7},... | collective-permute-start | bytes 196616 | tf_op jit(solution)/shard_map/ppermute | solution.py:238
  27.3 0.6 collective-permute-start.11
  27.9 0.8 %dynamic_slice.156 = f32[256]{0:T(256)S(1)} dynamic-slice(f32[2048]{0:T(1024)} %param.12, s32[]{:T(128)S(6)} %select_n.49), dynamic_slice_sizes={256} | dynamic-slice | bytes 2052 | tf_op jit(solution)/shard_map/dynamic_slice | solution.py:243
  28.6 0.1 copy.9.skip_ref
  28.8 2.6 %collective-permute-start.14 = (bf16[256,128]{1,0:T(8,128)(2,1)S(1)}, bf16[256,128]{1,0:T(8,128)(2,1)S(1)}, u32[]{:S(2)}, u32[]{:S(2)}) collective-permute-start(bf16[256,128]{1,0:T(8,128)(2,1)S(1)} %get-tuple-element.31), channel_id=1, source_target_pairs={{0,12},{2,14},{4,8},{6,10},{8,4},{10,6},{12,0},{14,2},{1,13},{3,15... | collective-permute-start | bytes 196616 | tf_op jit(solution)/shard_map/ppermute | solution.py:238
  31.4 1.0 %shard_map.84 = bf16[256,128]{1,0:T(8,128)(2,1)S(1)} custom-call(s32[2]{0:T(128)S(1)} %pad_add_fusion.me_ref, bf16[2048,128]{1,0:T(8,128)(2,1)S(1)} %collective-permute-done.8.halo_ref, bf16[1024,256]{1,0:T(8,128)(2,1)S(1)} %copy-done.1, bf16[256,128]{1,0:T(8,128)(2,1)S(1)} %get-tuple-element.67.refs_0_, bf16[256,128]{1,0:T(8,128)(2,1)S(1)} %get-tuple-element.89.refs_1_, ...), custom_call_target="tpu_custom_call" | custom-call | flops 268435456 | bytes 1245192 | tf_op jit(solution)/shard_map/pallas_call | solution.py:200
  32.4 0.0 collective-permute-done.7.other_ref
  32.4 0.7 %collective-permute-start.15 = (bf16[256,128]{1,0:T(8,128)(2,1)S(1)}, bf16[256,128]{1,0:T(8,128)(2,1)S(1)}, u32[]{:S(2)}, u32[]{:S(2)}) collective-permute-start(bf16[256,128]{1,0:T(8,128)(2,1)S(1)} %get-tuple-element.32), channel_id=1, source_target_pairs={{0,14},{2,12},{4,10},{6,8},{8,6},{10,4},{12,2},{14,0},{1,15},{3,13... | collective-permute-start | bytes 196616 | tf_op jit(solution)/shard_map/ppermute | solution.py:238
  33.1 0.0 collective-permute-done.10.refs_2_
  33.1 0.7 %collective-permute-start.9 = (bf16[256,128]{1,0:T(8,128)(2,1)S(1)}, bf16[256,128]{1,0:T(8,128)(2,1)S(1)}, u32[]{:S(2)}, u32[]{:S(2)}) collective-permute-start(bf16[256,128]{1,0:T(8,128)(2,1)S(1)} %get-tuple-element.28), channel_id=1, source_target_pairs={{0,2},{2,0},{4,6},{6,4},{8,10},{10,8},{12,14},{14,12},{1,3},{3,1},... | collective-permute-start | bytes 196616 | tf_op jit(solution)/shard_map/ppermute | solution.py:238
  33.8 0.0 collective-permute-done.11.refs_3_
  33.8 0.7 %collective-permute-start.12 = (bf16[256,128]{1,0:T(8,128)(2,1)S(1)}, bf16[256,128]{1,0:T(8,128)(2,1)S(1)}, u32[]{:S(2)}, u32[]{:S(2)}) collective-permute-start(bf16[256,128]{1,0:T(8,128)(2,1)S(1)} %shard_map.84), channel_id=1, source_target_pairs={{0,8},{2,10},{4,12},{6,14},{8,0},{10,2},{12,4},{14,6},{1,9},{3,11}... | collective-permute-start | bytes 196616 | tf_op jit(solution)/shard_map/ppermute | solution.py:238
  34.6 3.1 %shard_map.83.refs_8_.filt_ref = f32[8,256,256]{2,1,0:T(8,128)S(1)} custom-call(s32[2]{0:T(128)S(1)} %pad_add_fusion.me_ref, bf16[8,128,128]{2,1,0:T(8,128)(2,1)S(1)} %bitcast_dynamic-update-slice_fusion.mine_ref, bf16[8,128,128]{2,1,0:T(8,128)(2,1)S(1)} %collective-permute-done.7.other_ref, bf16[256,128]{1,0:T(8,128)(2,1)S(1)} %constant_dynamic-slice_fusion.11.taps_ref, ...), custom_call_target="tpu_custom_call" | custom-call | flops 1610612736 | bytes 1115144 | tf_op jit(solution)/shard_map/pallas_call | solution.py:200
  37.7 0.0 collective-permute-done.13.refs_5_
  37.7 0.0 collective-permute-done.14.refs_6_
  37.7 1.0 %collective-permute-done.15.refs_7_ = bf16[256,128]{1,0:T(8,128)(2,1)S(1)} collective-permute-done((bf16[256,128]{1,0:T(8,128)(2,1)S(1)}, bf16[256,128]{1,0:T(8,128)(2,1)S(1)}, u32[]{:S(2)}, u32[]{:S(2)}) %collective-permute-start.15) | collective-permute-done | bytes 65568 | tf_op jit(solution)/shard_map/ppermute | solution.py:238
  38.7 0.0 collective-permute-done.9.refs_1_
  38.7 2.7 %collective-permute-done.12.refs_4_ = bf16[256,128]{1,0:T(8,128)(2,1)S(1)} collective-permute-done((bf16[256,128]{1,0:T(8,128)(2,1)S(1)}, bf16[256,128]{1,0:T(8,128)(2,1)S(1)}, u32[]{:S(2)}, u32[]{:S(2)}) %collective-permute-start.12) | collective-permute-done | bytes 65568 | tf_op jit(solution)/shard_map/ppermute | solution.py:238
  41.5 1.9 %shard_map.85 = (bf16[256,128]{1,0:T(8,128)(2,1)S(1)}, f32[8,256,256]{2,1,0:T(8,128)S(1)}) custom-call(s32[2]{0:T(128)S(1)} %pad_add_fusion.me_ref, bf16[256,128]{1,0:T(8,128)(2,1)S(1)} %get-tuple-element.27.refs_0_, bf16[256,128]{1,0:T(8,128)(2,1)S(1)} %collective-permute-done.9.refs_1_, bf16[256,128]{1,0:T(8,128)(2,1)S(1)} %collective-permute-done.10.refs_2_, ...), custom_call_target="tpu_custom_call" | custom-call | flops 805306368 | bytes 3145736 | tf_op jit(solution)/shard_map/pallas_call | solution.py:200
  43.3 0.0 copy-start.2
  43.4 2.6 %shard_map.86 = (bf16[256,128]{1,0:T(8,128)(2,1)S(1)}, bf16[256,128]{1,0:T(8,128)(2,1)S(1)}, bf16[256,128]{1,0:T(8,128)(2,1)S(1)}, bf16[256,128]{1,0:T(8,128)(2,...) custom-call(s32[2]{0:T(128)S(1)} %pad_add_fusion.me_ref, ...), custom_call_target="tpu_custom_call" | custom-call | flops 805306368 | bytes 4718600 | tf_op jit(solution)/shard_map/pallas_call | solution.py:200
  46.0 0.2 collective-permute-start.16
  46.1 0.0 collective-permute-start.17
  46.1 2.0 %collective-permute-start.18 = (bf16[256,128]{1,0:T(8,128)(2,1)S(1)}, bf16[256,128]{1,0:T(8,128)(2,1)S(1)}, u32[]{:S(2)}, u32[]{:S(2)}) collective-permute-start(bf16[256,128]{1,0:T(8,128)(2,1)S(1)} %get-tuple-element.37), channel_id=1, source_target_pairs={{0,4},{2,6},{4,0},{6,2},{8,12},{10,14},{12,8},{14,10},{1,5},{3,7},... | collective-permute-start | bytes 196616 | tf_op jit(solution)/shard_map/ppermute | solution.py:238
  48.2 1.0 %collective-permute-start.19 = (bf16[256,128]{1,0:T(8,128)(2,1)S(1)}, bf16[256,128]{1,0:T(8,128)(2,1)S(1)}, u32[]{:S(2)}, u32[]{:S(2)}) collective-permute-start(bf16[256,128]{1,0:T(8,128)(2,1)S(1)} %get-tuple-element.38), channel_id=1, source_target_pairs={{0,14},{2,12},{4,10},{6,8},{8,6},{10,4},{12,2},{14,0},{1,15},{3,13... | collective-permute-start | bytes 196616 | tf_op jit(solution)/shard_map/ppermute | solution.py:238
  49.2 2.2 %collective-permute-start.20 = (bf16[256,128]{1,0:T(8,128)(2,1)S(1)}, bf16[256,128]{1,0:T(8,128)(2,1)S(1)}, u32[]{:S(2)}, u32[]{:S(2)}) collective-permute-start(bf16[256,128]{1,0:T(8,128)(2,1)S(1)} %get-tuple-element.39), channel_id=1, source_target_pairs={{0,12},{2,14},{4,8},{6,10},{8,4},{10,6},{12,0},{14,2},{1,13},{3,15... | collective-permute-start | bytes 196616 | tf_op jit(solution)/shard_map/ppermute | solution.py:238
  51.4 0.0 collective-permute-done.16.refs_1_
  51.4 0.0 collective-permute-start.21
  51.4 0.0 collective-permute-done.17.refs_2_
  51.4 2.9 %collective-permute-start.22 = (bf16[256,128]{1,0:T(8,128)(2,1)S(1)}, bf16[256,128]{1,0:T(8,128)(2,1)S(1)}, u32[]{:S(2)}, u32[]{:S(2)}) collective-permute-start(bf16[256,128]{1,0:T(8,128)(2,1)S(1)} %get-tuple-element.41), channel_id=1, source_target_pairs={{0,8},{2,10},{4,12},{6,14},{8,0},{10,2},{12,4},{14,6},{1,9},{3,11}... | collective-permute-start | bytes 196616 | tf_op jit(solution)/shard_map/ppermute | solution.py:238
  54.4 0.0 copy-done.2
  54.4 0.0 collective-permute-done.18.refs_3_
  54.4 0.0 collective-permute-done.19.refs_4_
  54.5 1.6 %collective-permute-done.20.refs_5_ = bf16[256,128]{1,0:T(8,128)(2,1)S(1)} collective-permute-done((bf16[256,128]{1,0:T(8,128)(2,1)S(1)}, bf16[256,128]{1,0:T(8,128)(2,1)S(1)}, u32[]{:S(2)}, u32[]{:S(2)}) %collective-permute-start.20) | collective-permute-done | bytes 65568 | tf_op jit(solution)/shard_map/ppermute | solution.py:238
  56.0 4.2 %collective-permute-done.21.refs_6_ = bf16[256,128]{1,0:T(8,128)(2,1)S(1)} collective-permute-done((bf16[256,128]{1,0:T(8,128)(2,1)S(1)}, bf16[256,128]{1,0:T(8,128)(2,1)S(1)}, u32[]{:S(2)}, u32[]{:S(2)}) %collective-permute-start.21) | collective-permute-done | bytes 65568 | tf_op jit(solution)/shard_map/ppermute | solution.py:238
  60.2 1.7 %collective-permute-done.22.refs_7_ = bf16[256,128]{1,0:T(8,128)(2,1)S(1)} collective-permute-done((bf16[256,128]{1,0:T(8,128)(2,1)S(1)}, bf16[256,128]{1,0:T(8,128)(2,1)S(1)}, u32[]{:S(2)}, u32[]{:S(2)}) %collective-permute-start.22) | collective-permute-done | bytes 65568 | tf_op jit(solution)/shard_map/ppermute | solution.py:238
  61.9 1.4 %shard_map.87 = bf16[2048,128]{1,0:T(8,128)(2,1)} custom-call(s32[2]{0:T(128)S(1)} %pad_add_fusion.me_ref, bf16[256,128]{1,0:T(8,128)(2,1)S(1)} %get-tuple-element.34.refs_0_, bf16[256,128]{1,0:T(8,128)(2,1)S(1)} %collective-permute-done.16.refs_1_, bf16[256,128]{1,0:T(8,128)(2,1)S(1)} %collective-permute-done.17.refs_2_, ...), custom_call_target="tpu_custom_call" | custom-call | flops 262144 | bytes 1048584 | tf_op jit(solution)/shard_map/pallas_call | solution.py:200
  (14 shorter events, 0.1 us)
Async XLA Ops:
  0.0 27.9 %copy-start = (bf16[2048,128]{1,0:T(8,128)(2,1)S(1)}, bf16[2048,128]{1,0:T(8,128)(2,1)}, u32[]{:S(2)}) copy-start(bf16[2048,128]{1,0:T(8,128)(2,1)} %param.13) | copy-start | bytes 1572868
  0.0 12.2 %copy-start.3 = (bf16[2048,128]{1,0:T(8,128)(2,1)S(1)}, bf16[2048,128]{1,0:T(8,128)(2,1)}, u32[]{:S(2)}) copy-start(bf16[2048,128]{1,0:T(8,128)(2,1)} %param.10) | copy-start | bytes 1572868
  0.0 12.2 %copy-start.4 = (bf16[2048,128]{1,0:T(8,128)(2,1)S(1)}, bf16[2048,128]{1,0:T(8,128)(2,1)}, u32[]{:S(2)}) copy-start(bf16[2048,128]{1,0:T(8,128)(2,1)} %param.9) | copy-start | bytes 1572868
  0.0 21.7 %collective-permute-start.8 = (bf16[2048,128]{1,0:T(8,128)(2,1)}, bf16[2048,128]{1,0:T(8,128)(2,1)S(1)}, u32[]{:S(2)}, u32[]{:S(2)}) collective-permute-start(bf16[2048,128]{1,0:T(8,128)(2,1)} %param.8), channel_id=1, source_target_pairs={{0,2},{2,4},{4,6},{6,8},{8,10},{10,12},{12,14},{1,3},{3,5},{5,7},{... | collective-permute-start | bytes 1572872 | tf_op jit(solution)/shard_map/ppermute | solution.py:240
  2.6 19.1 %copy-start.1 = (bf16[1024,256]{1,0:T(8,128)(2,1)S(1)}, bf16[1024,256]{1,0:T(8,128)(2,1)}, u32[]{:S(2)}) copy-start(bf16[1024,256]{1,0:T(8,128)(2,1)} %constant.37.clone.table_ref.refs_9_) | copy-start | bytes 1572868
  3.6 8.8 %collective-permute-start = (bf16[128,128]{1,0:T(8,128)(2,1)S(1)}, bf16[128,128]{1,0:T(8,128)(2,1)S(1)}, u32[]{:S(2)}, u32[]{:S(2)}) collective-permute-start(bf16[128,128]{1,0:T(8,128)(2,1)S(1)} %get-tuple-element.81), channel_id=1, source_target_pairs={{0,2},{2,0},{4,6},{6,4},{8,10},{10,8},{12,14},{14,12},{1,3},{3,1},... | collective-permute-start | bytes 98312 | tf_op jit(solution)/shard_map/ppermute | solution.py:238
  6.3 6.5 %collective-permute-start.1 = (bf16[128,128]{1,0:T(8,128)(2,1)S(1)}, bf16[128,128]{1,0:T(8,128)(2,1)S(1)}, u32[]{:S(2)}, u32[]{:S(2)}) collective-permute-start(bf16[128,128]{1,0:T(8,128)(2,1)S(1)} %get-tuple-element.80), channel_id=1, source_target_pairs={{0,4},{2,6},{4,0},{6,2},{8,12},{10,14},{12,8},{14,10},{1,5},{3,7},... | collective-permute-start | bytes 98312 | tf_op jit(solution)/shard_map/ppermute | solution.py:238
  7.9 7.0 %collective-permute-start.2 = (bf16[128,128]{1,0:T(8,128)(2,1)S(1)}, bf16[128,128]{1,0:T(8,128)(2,1)S(1)}, u32[]{:S(2)}, u32[]{:S(2)}) collective-permute-start(bf16[128,128]{1,0:T(8,128)(2,1)S(1)} %get-tuple-element.79), channel_id=1, source_target_pairs={{0,6},{2,4},{4,2},{6,0},{8,14},{10,12},{12,10},{14,8},{1,7},{3,5},... | collective-permute-start | bytes 98312 | tf_op jit(solution)/shard_map/ppermute | solution.py:238
  7.9 9.3 %collective-permute-start.3 = (bf16[128,128]{1,0:T(8,128)(2,1)S(1)}, bf16[128,128]{1,0:T(8,128)(2,1)S(1)}, u32[]{:S(2)}, u32[]{:S(2)}) collective-permute-start(bf16[128,128]{1,0:T(8,128)(2,1)S(1)} %get-tuple-element.78), channel_id=1, source_target_pairs={{0,8},{2,10},{4,12},{6,14},{8,0},{10,2},{12,4},{14,6},{1,9},{3,11}... | collective-permute-start | bytes 98312 | tf_op jit(solution)/shard_map/ppermute | solution.py:238
  12.4 5.2 %collective-permute-start.4 = (bf16[128,128]{1,0:T(8,128)(2,1)S(1)}, bf16[128,128]{1,0:T(8,128)(2,1)S(1)}, u32[]{:S(2)}, u32[]{:S(2)}) collective-permute-start(bf16[128,128]{1,0:T(8,128)(2,1)S(1)} %get-tuple-element.77), channel_id=1, source_target_pairs={{0,10},{2,8},{4,14},{6,12},{8,2},{10,0},{12,6},{14,4},{1,11},{3,9}... | collective-permute-start | bytes 98312 | tf_op jit(solution)/shard_map/ppermute | solution.py:238
  12.8 6.1 %collective-permute-start.5 = (bf16[128,128]{1,0:T(8,128)(2,1)S(1)}, bf16[128,128]{1,0:T(8,128)(2,1)S(1)}, u32[]{:S(2)}, u32[]{:S(2)}) collective-permute-start(bf16[128,128]{1,0:T(8,128)(2,1)S(1)} %get-tuple-element.76), channel_id=1, source_target_pairs={{0,12},{2,14},{4,8},{6,10},{8,4},{10,6},{12,0},{14,2},{1,13},{3,15... | collective-permute-start | bytes 98312 | tf_op jit(solution)/shard_map/ppermute | solution.py:238
  14.9 5.3 %collective-permute-start.6 = (bf16[128,128]{1,0:T(8,128)(2,1)S(1)}, bf16[128,128]{1,0:T(8,128)(2,1)S(1)}, u32[]{:S(2)}, u32[]{:S(2)}) collective-permute-start(bf16[128,128]{1,0:T(8,128)(2,1)S(1)} %get-tuple-element.75), channel_id=1, source_target_pairs={{0,14},{2,12},{4,10},{6,8},{8,6},{10,4},{12,2},{14,0},{1,15},{3,13... | collective-permute-start | bytes 98312 | tf_op jit(solution)/shard_map/ppermute | solution.py:238
  20.2 12.2 %collective-permute-start.7 = (bf16[8,128,128]{2,1,0:T(8,128)(2,1)S(1)}, bf16[8,128,128]{2,1,0:T(8,128)(2,1)S(1)}, u32[]{:S(2)}, u32[]{:S(2)}) collective-permute-start(bf16[8,128,128]{2,1,0:T(8,128)(2,1)S(1)} %bitcast_dynamic-update-slice_fusion.mine_ref), channel_id=1, source_target_pairs={{0,16},{16,0},{1,17},{17,1},{2,18},{18,2},{3,19},{19,3},{4,20},{20... | collective-permute-start | bytes 786440 | tf_op jit(solution)/shard_map/ppermute | solution.py:253
  24.4 13.3 %collective-permute-start.13 = (bf16[256,128]{1,0:T(8,128)(2,1)S(1)}, bf16[256,128]{1,0:T(8,128)(2,1)S(1)}, u32[]{:S(2)}, u32[]{:S(2)}) collective-permute-start(bf16[256,128]{1,0:T(8,128)(2,1)S(1)} %get-tuple-element.24), channel_id=1, source_target_pairs={{0,10},{2,8},{4,14},{6,12},{8,2},{10,0},{12,6},{14,4},{1,11},{3,9}... | collective-permute-start | bytes 196616 | tf_op jit(solution)/shard_map/ppermute | solution.py:238
  24.5 8.7 %collective-permute-start.10 = (bf16[256,128]{1,0:T(8,128)(2,1)S(1)}, bf16[256,128]{1,0:T(8,128)(2,1)S(1)}, u32[]{:S(2)}, u32[]{:S(2)}) collective-permute-start(bf16[256,128]{1,0:T(8,128)(2,1)S(1)} %get-tuple-element.29), channel_id=1, source_target_pairs={{0,4},{2,6},{4,0},{6,2},{8,12},{10,14},{12,8},{14,10},{1,5},{3,7},... | collective-permute-start | bytes 196616 | tf_op jit(solution)/shard_map/ppermute | solution.py:238
  27.3 6.6 %collective-permute-start.11 = (bf16[256,128]{1,0:T(8,128)(2,1)S(1)}, bf16[256,128]{1,0:T(8,128)(2,1)S(1)}, u32[]{:S(2)}, u32[]{:S(2)}) collective-permute-start(bf16[256,128]{1,0:T(8,128)(2,1)S(1)} %get-tuple-element.30), channel_id=1, source_target_pairs={{0,6},{2,4},{4,2},{6,0},{8,14},{10,12},{12,10},{14,8},{1,7},{3,5},... | collective-permute-start | bytes 196616 | tf_op jit(solution)/shard_map/ppermute | solution.py:238
  28.8 8.9 %collective-permute-start.14 = (bf16[256,128]{1,0:T(8,128)(2,1)S(1)}, bf16[256,128]{1,0:T(8,128)(2,1)S(1)}, u32[]{:S(2)}, u32[]{:S(2)}) collective-permute-start(bf16[256,128]{1,0:T(8,128)(2,1)S(1)} %get-tuple-element.31), channel_id=1, source_target_pairs={{0,12},{2,14},{4,8},{6,10},{8,4},{10,6},{12,0},{14,2},{1,13},{3,15... | collective-permute-start | bytes 196616 | tf_op jit(solution)/shard_map/ppermute | solution.py:238
  32.4 6.3 %collective-permute-start.15 = (bf16[256,128]{1,0:T(8,128)(2,1)S(1)}, bf16[256,128]{1,0:T(8,128)(2,1)S(1)}, u32[]{:S(2)}, u32[]{:S(2)}) collective-permute-start(bf16[256,128]{1,0:T(8,128)(2,1)S(1)} %get-tuple-element.32), channel_id=1, source_target_pairs={{0,14},{2,12},{4,10},{6,8},{8,6},{10,4},{12,2},{14,0},{1,15},{3,13... | collective-permute-start | bytes 196616 | tf_op jit(solution)/shard_map/ppermute | solution.py:238
  33.1 5.6 %collective-permute-start.9 = (bf16[256,128]{1,0:T(8,128)(2,1)S(1)}, bf16[256,128]{1,0:T(8,128)(2,1)S(1)}, u32[]{:S(2)}, u32[]{:S(2)}) collective-permute-start(bf16[256,128]{1,0:T(8,128)(2,1)S(1)} %get-tuple-element.28), channel_id=1, source_target_pairs={{0,2},{2,0},{4,6},{6,4},{8,10},{10,8},{12,14},{14,12},{1,3},{3,1},... | collective-permute-start | bytes 196616 | tf_op jit(solution)/shard_map/ppermute | solution.py:238
  33.8 7.6 %collective-permute-start.12 = (bf16[256,128]{1,0:T(8,128)(2,1)S(1)}, bf16[256,128]{1,0:T(8,128)(2,1)S(1)}, u32[]{:S(2)}, u32[]{:S(2)}) collective-permute-start(bf16[256,128]{1,0:T(8,128)(2,1)S(1)} %shard_map.84), channel_id=1, source_target_pairs={{0,8},{2,10},{4,12},{6,14},{8,0},{10,2},{12,4},{14,6},{1,9},{3,11}... | collective-permute-start | bytes 196616 | tf_op jit(solution)/shard_map/ppermute | solution.py:238
  43.3 11.0 %copy-start.2 = (bf16[2048,128]{1,0:T(8,128)(2,1)S(1)}, bf16[2048,128]{1,0:T(8,128)(2,1)}, u32[]{:S(2)}) copy-start(bf16[2048,128]{1,0:T(8,128)(2,1)} %param.14) | copy-start | bytes 1572868
  46.0 5.4 %collective-permute-start.16 = (bf16[256,128]{1,0:T(8,128)(2,1)S(1)}, bf16[256,128]{1,0:T(8,128)(2,1)S(1)}, u32[]{:S(2)}, u32[]{:S(2)}) collective-permute-start(bf16[256,128]{1,0:T(8,128)(2,1)S(1)} %get-tuple-element.35), channel_id=1, source_target_pairs={{0,2},{2,0},{4,6},{6,4},{8,10},{10,8},{12,14},{14,12},{1,3},{3,1},... | collective-permute-start | bytes 196616 | tf_op jit(solution)/shard_map/ppermute | solution.py:238
  46.1 5.3 %collective-permute-start.17 = (bf16[256,128]{1,0:T(8,128)(2,1)S(1)}, bf16[256,128]{1,0:T(8,128)(2,1)S(1)}, u32[]{:S(2)}, u32[]{:S(2)}) collective-permute-start(bf16[256,128]{1,0:T(8,128)(2,1)S(1)} %get-tuple-element.36), channel_id=1, source_target_pairs={{0,6},{2,4},{4,2},{6,0},{8,14},{10,12},{12,10},{14,8},{1,7},{3,5},... | collective-permute-start | bytes 196616 | tf_op jit(solution)/shard_map/ppermute | solution.py:238
  46.1 8.3 %collective-permute-start.18 = (bf16[256,128]{1,0:T(8,128)(2,1)S(1)}, bf16[256,128]{1,0:T(8,128)(2,1)S(1)}, u32[]{:S(2)}, u32[]{:S(2)}) collective-permute-start(bf16[256,128]{1,0:T(8,128)(2,1)S(1)} %get-tuple-element.37), channel_id=1, source_target_pairs={{0,4},{2,6},{4,0},{6,2},{8,12},{10,14},{12,8},{14,10},{1,5},{3,7},... | collective-permute-start | bytes 196616 | tf_op jit(solution)/shard_map/ppermute | solution.py:238
  48.2 6.3 %collective-permute-start.19 = (bf16[256,128]{1,0:T(8,128)(2,1)S(1)}, bf16[256,128]{1,0:T(8,128)(2,1)S(1)}, u32[]{:S(2)}, u32[]{:S(2)}) collective-permute-start(bf16[256,128]{1,0:T(8,128)(2,1)S(1)} %get-tuple-element.38), channel_id=1, source_target_pairs={{0,14},{2,12},{4,10},{6,8},{8,6},{10,4},{12,2},{14,0},{1,15},{3,13... | collective-permute-start | bytes 196616 | tf_op jit(solution)/shard_map/ppermute | solution.py:238
  49.2 6.8 %collective-permute-start.20 = (bf16[256,128]{1,0:T(8,128)(2,1)S(1)}, bf16[256,128]{1,0:T(8,128)(2,1)S(1)}, u32[]{:S(2)}, u32[]{:S(2)}) collective-permute-start(bf16[256,128]{1,0:T(8,128)(2,1)S(1)} %get-tuple-element.39), channel_id=1, source_target_pairs={{0,12},{2,14},{4,8},{6,10},{8,4},{10,6},{12,0},{14,2},{1,13},{3,15... | collective-permute-start | bytes 196616 | tf_op jit(solution)/shard_map/ppermute | solution.py:238
  51.4 8.8 %collective-permute-start.21 = (bf16[256,128]{1,0:T(8,128)(2,1)S(1)}, bf16[256,128]{1,0:T(8,128)(2,1)S(1)}, u32[]{:S(2)}, u32[]{:S(2)}) collective-permute-start(bf16[256,128]{1,0:T(8,128)(2,1)S(1)} %get-tuple-element.40), channel_id=1, source_target_pairs={{0,10},{2,8},{4,14},{6,12},{8,2},{10,0},{12,6},{14,4},{1,11},{3,9}... | collective-permute-start | bytes 196616 | tf_op jit(solution)/shard_map/ppermute | solution.py:238
  51.4 10.5 %collective-permute-start.22 = (bf16[256,128]{1,0:T(8,128)(2,1)S(1)}, bf16[256,128]{1,0:T(8,128)(2,1)S(1)}, u32[]{:S(2)}, u32[]{:S(2)}) collective-permute-start(bf16[256,128]{1,0:T(8,128)(2,1)S(1)} %get-tuple-element.41), channel_id=1, source_target_pairs={{0,8},{2,10},{4,12},{6,14},{8,0},{10,2},{12,4},{14,6},{1,9},{3,11}... | collective-permute-start | bytes 196616 | tf_op jit(solution)/shard_map/ppermute | solution.py:238

commit v3 on v2

--- a/solution.py
+++ b/solution.py
@@ -76,30 +76,49 @@
     return pl.ds(pl.multiple_of(index * rows, rows), rows)
 
 
-def first_kernel(which, me_ref, halo_ref, table_ref, *refs):
+def prep_kernel(shards, table_ref, *refs):
+    own_hat, taps_hat = refs[2 * shards :]
+    hi, lo, top, _ = parts_of(table_ref)
+    n = hi.shape[0] // 2
+    bottom = jnp.concatenate([hi[n:], lo[n:]], axis=0)
+    for k in range(shards):
+        own_hat[k] = block_spectrum(refs[2 * k][...], bottom)
+        taps_hat[k] = block_spectrum(refs[2 * k + 1][...], top)
+
+
+def first_kernel(which, me_ref, halo_ref, table_ref, own_hat, taps_hat, *refs):
     count = len(which)
-    outs = refs[3 * count :]
+    gates, outs = refs[:count], refs[count:]
     rows = outs[0].shape[0]
     me = me_ref[0]
-    hi, lo, top, both = parts_of(table_ref)
+    _, _, top, both = parts_of(table_ref)
     for i, k in enumerate(which):
-        x_ref, gate_ref, taps_ref = refs[3 * i : 3 * i + 3]
-        spectrum = window_spectrum(halo_ref[rows_at(me ^ k, rows), :], x_ref[...], hi, lo)
-        taps = block_spectrum(taps_ref[...], top)
-        conv = valid_part(times(spectrum, taps), both)
-        outs[i][...] = (conv * gate_ref[...].astype(F32)).astype(BF16)
-
-
-def filter_kernel(shards, me_ref, mine_ref, other_ref, taps_ref, skip_ref, table_ref, out_ref, lags, taps_hat):
-    half = mine_ref.shape[1]
-    me, group = me_ref[0], me_ref[1]
+        spectrum = own_hat[k] + block_spectrum(halo_ref[rows_at(me ^ k, rows), :], top)
+        conv = valid_part(times(spectrum, taps_hat[k]), both)
+        outs[i][...] = (conv * gates[i][...].astype(F32)).astype(BF16)
+
+
+def filter_kernel(toks, me_ref, held_ref, first_ref, second_ref, taps_ref, skip_ref, table_ref, out_ref, lags, taps_hat):
+    tok, sec, group = me_ref[1], me_ref[2], me_ref[3]
     hi, lo, top, both = parts_of(table_ref)
     lags[0] = jnp.zeros(lags.shape[1:], BF16)
-    for k in range(shards):
-        lags[(me ^ k) + 1, rows_at(group, half), :] = mine_ref[k]
-        lags[(me ^ k) + 1, rows_at(1 - group, half), :] = other_ref[k]
+
+    def fill(same_ref, other_ref):
+        for k in range(toks):
+            at = (tok ^ k) * 2 + 1
+            lags[at + sec] = same_ref[k]
+            lags[at + 1 - sec] = other_ref[k]
+
+    @pl.when(sec == group)
+    def _():
+        fill(held_ref, first_ref)
+
+    @pl.when(sec != group)
+    def _():
+        fill(first_ref, second_ref)
+
     taps_hat[...] = block_spectrum(taps_ref[...], top)
-    for m in range(shards):
+    for m in range(2 * toks):
         spectrum = window_spectrum(lags[m], lags[m + 1], hi, lo)
         joined = valid_part(times(spectrum, taps_hat[...]), both)
         part_hi, part_lo = two_parts(joined)
@@ -110,18 +129,8 @@
         out_ref[m] = result
 
 
-def lead_kernel(shards, lead, me_ref, *refs):
-    pieces = refs[:shards]
-    filt_ref, table_ref, out_ref, spectra, signal, total = refs[shards:]
-    rows, block = pieces[0].shape
-    me = me_ref[0]
-    hi, lo, _, both = parts_of(table_ref)
-    signal[0] = jnp.zeros((rows, block), BF16)
-    for k in range(shards):
-        signal[(me ^ k) + 1] = pieces[k][...]
-    for j in range(shards):
-        spectra[j] = window_spectrum(signal[j], signal[j + 1], hi, lo)
-    j = me ^ lead
+def one_block(j, filt_ref, spectra, both, out_ref, total):
+    rows, block = out_ref.shape
     tile = min(64, rows)
 
     def row_tile(i, carry):
@@ -140,6 +149,19 @@
 
     lax.fori_loop(0, rows // tile, row_tile, 0)
     out_ref[...] = valid_part(total[...], both).astype(BF16)
+
+
+def lead_kernel(shards, lead, me_ref, *refs):
+    pieces = refs[:shards]
+    filt_ref, table_ref, out_ref, spectra, signal, total = refs[shards:]
+    me = me_ref[0]
+    hi, lo, _, both = parts_of(table_ref)
+    signal[0] = jnp.zeros(signal.shape[1:], BF16)
+    for k in range(shards):
+        signal[(me ^ k) + 1] = pieces[k][...]
+    for j in range(shards):
+        spectra[j] = window_spectrum(signal[j], signal[j + 1], hi, lo)
+    one_block(me ^ lead, filt_ref, spectra, both, out_ref, total)
 
 
 def long_kernel(shards, which, me_ref, filt_ref, spectra, table_ref, *refs):
@@ -186,6 +208,7 @@
         copy.wait()
 
 
+SMEM = pl.BlockSpec(memory_space=pltpu.SMEM)
 VMEM = pl.BlockSpec(memory_space=pltpu.VMEM)
 HBM = pl.BlockSpec(memory_space=pltpu.HBM)
 
@@ -200,7 +223,7 @@
     return pl.pallas_call(
         kernel,
         out_shape=out_shape,
-        in_specs=[pl.BlockSpec(memory_space=pltpu.SMEM)] + [in_space] * (len(inputs) - 1),
+        in_specs=[SMEM if a.dtype == jnp.int32 else in_space for a in inputs],
         out_specs=[out_space] * len(out_shape) if many else out_space,
         scratch_shapes=list(scratch),
         compiler_params=pltpu.CompilerParams(vmem_limit_bytes=limit),
@@ -219,14 +242,15 @@
 
 def stages(features, gate_one, taps_one, long_filter, skip_gain, taps_two, gate_two):
     shards = lax.axis_size(AXES)
-    groups = lax.axis_size("grp")
-    assert shards & (shards - 1) == 0 and groups == 2
+    toks = lax.axis_size("tok")
+    assert shards & (shards - 1) == 0
+    assert lax.axis_size("grp") == 2 and lax.axis_size("sec") == 2
     channels, block = features.shape
     assert taps_one.shape[1] == block and taps_two.shape[1] == block
     narrow = channels // shards
-    half = narrow // groups
     me = lax.axis_index(AXES)
-    place = jnp.stack([me, lax.axis_index("grp")]).astype(jnp.int32)
+    tok, sec, group = (lax.axis_index(name) for name in ("tok", "sec", "grp"))
+    place = jnp.stack([me, tok, sec, group]).astype(jnp.int32)
     flops = 2 * channels * 256 * 256
     order = far_first(shards)
     lead = order[0]
@@ -243,34 +267,40 @@
         return lax.dynamic_slice_in_dim(array, (me ^ k) * narrow, narrow)
 
     table = tables(block)
-    by_owner = long_filter.reshape(shards, groups, half, block)
-    group = lax.axis_index("grp")
+    spectrum = jax.ShapeDtypeStruct((shards, narrow, 2 * block), F32)
+
     lags = [
-        lax.dynamic_slice(by_owner, (me ^ k, group, 0, 0), (1, 1, half, block)).reshape(half, block)
-        for k in range(shards)
+        lax.dynamic_slice_in_dim(long_filter, ((tok ^ k) * 2 + group) * narrow, narrow)
+        for k in range(toks)
     ]
-    mine = jnp.stack([swapped(lags[k], k) for k in range(shards)])
-    other = lax.ppermute(mine, "grp", [(0, 1), (1, 0)])
+    cuts = {k: [rows_for(a, k) for a in (features, gate_one, taps_one)] for k in range(shards)}
+    skip_local, taps_local = rows_for(skip_gain, 0)[:, None], rows_for(taps_two, 0)
+    lags, cuts, skip_local, taps_local = lax.optimization_barrier((lags, cuts, skip_local, taps_local))
+    for k in range(1, toks):
+        lags[k] = lax.ppermute(lags[k], "tok", [(i, i ^ k) for i in range(toks)])
+    held = jnp.stack(lags)
+    own_hat, taps_hat = call(
+        functools.partial(prep_kernel, shards),
+        (table, *[piece for k in range(shards) for piece in (cuts[k][0], cuts[k][2])]),
+        [spectrum, spectrum],
+        flops=2 * flops,
+    )
+    first = lax.ppermute(held, ("grp", "sec"), [(0, 2), (3, 1), (1, 0), (2, 3)])
+    second = lax.ppermute(held, ("grp", "sec"), [(1, 2), (2, 1)])
 
     piece = jax.ShapeDtypeStruct((narrow, block), BF16)
 
     def operands(which):
-        cuts = []
-        for k in which:
-            cuts += [rows_for(features, k), rows_for(gate_one, k), rows_for(taps_one, k)]
-        return (place, halo, table, *cuts)
+        return (place, halo, table, own_hat, taps_hat, *[cuts[k][1] for k in which])
 
     (front,) = call(functools.partial(first_kernel, [lead]), operands([lead]), [piece], flops=flops)
     others = call(functools.partial(first_kernel, rest), operands(rest), [piece] * len(rest), flops=6 * flops)
     mixed = {k: swapped(p, k) for k, p in zip([lead] + rest, [front] + list(others))}
 
-    skip_late, taps_late, gate_late, _ = lax.optimization_barrier((skip_gain, taps_two, gate_two, others[0]))
-    skip_local = rows_for(skip_late, 0)[:, None]
-    taps_local = rows_for(taps_late, 0)
-    spectrum = jax.ShapeDtypeStruct((shards, narrow, 2 * block), F32)
+    gate_late, _ = lax.optimization_barrier((gate_two, others[0]))
     joined = call(
-        functools.partial(filter_kernel, shards),
-        (place, mine, other, taps_local, skip_local, table),
+        functools.partial(filter_kernel, toks),
+        (place, held, first, second, taps_local, skip_local, table),
         spectrum,
         scratch=[
             pltpu.VMEM((shards + 1, narrow, block), BF16),

time: 63.6 us -> 63.3 us (level)
  waiting for transfers between devices: 14.2 us -> 16.7 us
  starting transfers between devices: 32.2 us -> 29.8 us
  local copies, waits for them, and re-layouts: 3.94 us -> 3.22 us
    ppermute x21 -> x14, starting transfers between devices: 28.1 us -> 19.9 us  [swapped(): return lax.ppermute(piece, AXES, [(i, i ^ k) for i in range(shards)])]
    ppermute x1 -> x5, waiting for transfers between devices: 0.01 us -> 5.99 us  [the longest x3 5.98 us: stages(): lags[k] = lax.ppermute(lags[k], 'tok', [(i, i ^ k) for i in range(toks)])]
    ppermute x1 -> x5, starting transfers between devices: 1.52 us -> 7.4 us  [the longest x3 5.2 us: stages(): lags[k] = lax.ppermute(lags[k], 'tok', [(i, i ^ k) for i in range(toks)])]
    ppermute x21 -> x14, waiting for transfers between devices: 14.2 us -> 10.7 us  [swapped(): return lax.ppermute(piece, AXES, [(i, i ^ k) for i in range(shards)])]
    dynamic_slice x0 -> x1, local copies, waits for them, and re-layouts: none -> 1.01 us  [stages(): lax.dynamic_slice_in_dim(long_filter, ((tok ^ k) * 2 + group) * narrow, n...]
    reshape x1 -> x0, local copies, waits for them, and re-layouts: 0.94 us -> none  [stages(): lax.dynamic_slice(by_owner, (me ^ k, group, 0, 0), (1, 1, half, block))]
    unnamed x17 -> x8, local copies, waits for them, and re-layouts: 0.84 us -> 0.02 us
    pallas_call x6 -> x7, Pallas kernels: 12.6 us -> 12.9 us  [call(): pl.pallas_call(kernel, out_shape=out_shape, in_specs=[SMEM if a.dtype ==...]
  transfers between devices with their start and end apart: 23 -> 20, of which waited for: 8 -> 7; matrix products, arithmetic and copies ran while one was open for 6% -> 5% of each run, Pallas kernels for 11% -> 11%
where the time goes in v3:
time: 63.3 us; the launch traced here: 63.1 us
  starting transfers between devices  29.8 us (47%)
  waiting for transfers between devices  16.7 us (26%)
  Pallas kernels  12.9 us (20%)
  local copies, waits for them, and re-layouts  3.22 us (5%)
    ppermute x14, starting transfers between devices, swapped(): return lax.ppermute(piece, AXES, [(i, i ^ k) for i in range(shards)])  19.9 us
    pallas_call x7, Pallas kernels, call(): pl.pallas_call(kernel, out_shape=out_shape, in_specs=[SMEM if a.dtype ==...  12.9 us
    ppermute x14, waiting for transfers between devices, swapped(): return lax.ppermute(piece, AXES, [(i, i ^ k) for i in range(shards)])  10.7 us
    ppermute x3, waiting for transfers between devices, stages(): lags[k] = lax.ppermute(lags[k], 'tok', [(i, i ^ k) for i in range(toks)])  5.98 us
    ppermute x3, starting transfers between devices, stages(): lags[k] = lax.ppermute(lags[k], 'tok', [(i, i ^ k) for i in range(toks)])  5.2 us
    ppermute x1, starting transfers between devices, stages(): halo = lax.ppermute(features, AXES, [(i, i + 1) for i in range(shards - 1)])  2.55 us
    dynamic_slice x4, local copies, waits for them, and re-layouts, rows_for(): return lax.dynamic_slice_in_dim(array, (me ^ k) * narrow, narrow)  2.07 us
    ppermute x1, starting transfers between devices, stages(): first = lax.ppermute(held, ('grp', 'sec'), [(0, 2), (3, 1), (1, 0), (2, 3)])  1.54 us
  transfers between devices with their start and end apart: 20, of which 7 were waited for; matrix products, arithmetic and copies ran while one was open for 5% of the time, Pallas kernels for 11%

profile of v3, /device:TPU:0, one launch (start us, length us, event | category | flops | bytes accessed | tf_op | source)
XLA Modules:
  0.0 63.1 jit_solution(11249594146313415697)
XLA Ops:
  0.0 0.0 copy-start.2
  0.0 0.0 copy-start.3
  0.0 2.6 %collective-permute-start.5 = (bf16[2048,128]{1,0:T(8,128)(2,1)}, bf16[2048,128]{1,0:T(8,128)(2,1)S(1)}, u32[]{:S(2)}, u32[]{:S(2)}) collective-permute-start(bf16[2048,128]{1,0:T(8,128)(2,1)} %param.8), channel_id=1, source_target_pairs={{0,2},{2,4},{4,6},{6,8},{8,10},{10,12},{12,14},{1,3},{3,5},{5,7},{... | collective-permute-start | bytes 1572872 | tf_op jit(solution)/shard_map/ppermute | solution.py:264
  2.6 0.8 %dynamic_slice.142 = f32[256]{0:T(256)S(1)} dynamic-slice(f32[2048]{0:T(1024)} %param.12, s32[]{:T(128)S(6)} %select_n.28), dynamic_slice_sizes={256} | dynamic-slice | bytes 2052 | tf_op jit(solution)/shard_map/dynamic_slice | solution.py:267
  3.4 0.0 copy-start
  3.4 1.2 %constant_dynamic-slice_fusion.11 = (bf16[256,128]{1,0:T(8,128)(2,1)S(1)}, bf16[256,128]{1,0:T(8,128)(2,1)S(1)}, bf16[256,128]{1,0:T(8,128)(2,1)S(1)}, bf16[256,...) fusion(bf16[2048,128]{1,0:T(8,128)(2,1)} %param.8, ...), kind=kLoop, calls=%fused_computation.12 | loop fusion | bytes 1048608 | tf_op jit(solution)/shard_map/dynamic_slice | solution.py:267
  4.6 1.0 %constant_dynamic-slice_fusion.33 = (bf16[256,128]{1,0:T(8,128)(2,1)S(1)}, bf16[256,128]{1,0:T(8,128)(2,1)S(1)}, bf16[256,128]{1,0:T(8,128)(2,1)S(1)}, bf16[256,128]{1,0:T(8,128)(2,1)S(1)}, bf16[256,128]{1,0:T(8,128)(2,1)S(1)}) fusion(bf16[2048,128]{1,0:T(8,128)(2,1)} %param.11, s32[]{:T(128)S(6)} %select_n.27, s32[]{:T(128)S(6)} %select_n.25, ...), kind=kLoop, calls=%fused_computation.34 | loop fusion | bytes 655380 | tf_op jit(solution)/shard_map/dynamic_slice | solution.py:273
  5.6 0.0 copy-done.2
  5.6 0.0 copy-done.3
  5.6 0.1 constant_dynamic-slice_fusion.9
  5.7 2.6 %collective-permute-start = (bf16[256,128]{1,0:T(8,128)(2,1)S(1)}, bf16[256,128]{1,0:T(8,128)(2,1)S(1)}, u32[]{:S(2)}, u32[]{:S(2)}) collective-permute-start(bf16[256,128]{1,0:T(8,128)(2,1)S(1)} %get-tuple-element.55), channel_id=1, source_target_pairs={{0,4},{4,0},{8,12},{12,8},{1,5},{5,1},{9,13},{13,9},{2,6},{6,2},{1... | collective-permute-start | bytes 196616 | tf_op jit(solution)/shard_map/ppermute | solution.py:280
  8.3 2.6 %collective-permute-start.1 = (bf16[256,128]{1,0:T(8,128)(2,1)S(1)}, bf16[256,128]{1,0:T(8,128)(2,1)S(1)}, u32[]{:S(2)}, u32[]{:S(2)}) collective-permute-start(bf16[256,128]{1,0:T(8,128)(2,1)S(1)} %get-tuple-element.56), channel_id=1, source_target_pairs={{0,8},{4,12},{8,0},{12,4},{1,9},{5,13},{9,1},{13,5},{2,10},{6,14},... | collective-permute-start | bytes 196616 | tf_op jit(solution)/shard_map/ppermute | solution.py:280
  10.9 0.0 collective-permute-start.2
  10.9 0.1 pad_add_fusion.me_ref
  11.0 0.0 collective-permute-done
  11.0 4.9 %collective-permute-done.1 = bf16[256,128]{1,0:T(8,128)(2,1)S(1)} collective-permute-done((bf16[256,128]{1,0:T(8,128)(2,1)S(1)}, bf16[256,128]{1,0:T(8,128)(2,1)S(1)}, u32[]{:S(2)}, u32[]{:S(2)}) %collective-permute-start.1) | collective-permute-done | bytes 65568 | tf_op jit(solution)/shard_map/ppermute | solution.py:280
  15.9 1.0 %collective-permute-done.2 = bf16[256,128]{1,0:T(8,128)(2,1)S(1)} collective-permute-done((bf16[256,128]{1,0:T(8,128)(2,1)S(1)}, bf16[256,128]{1,0:T(8,128)(2,1)S(1)}, u32[]{:S(2)}, u32[]{:S(2)}) %collective-permute-start.2) | collective-permute-done | bytes 65568 | tf_op jit(solution)/shard_map/ppermute | solution.py:280
  17.0 1.5 %collective-permute-start.3 = (bf16[4,256,128]{2,1,0:T(8,128)(2,1)S(1)}, bf16[4,256,128]{2,1,0:T(8,128)(2,1)S(1)}, u32[]{:S(2)}, u32[]{:S(2)}) collective-permute-start(bf16[4,256,128]{2,1,0:T(8,128)(2,1)S(1)} %pad_maximum_fusion.held_ref), channel_id=1, source_target_pairs={{0,16},{18,2},{2,0},{16,18},{1,17},{19,3},{3,1},{17,19},{4,20},{22... | collective-permute-start | bytes 786440 | tf_op jit(solution)/shard_map/ppermute | solution.py:288
  18.6 0.7 %collective-permute-start.4 = (bf16[4,256,128]{2,1,0:T(8,128)(2,1)S(1)}, bf16[4,256,128]{2,1,0:T(8,128)(2,1)S(1)}, u32[]{:S(2)}, u32[]{:S(2)}) collective-permute-start(bf16[4,256,128]{2,1,0:T(8,128)(2,1)S(1)} %pad_maximum_fusion.held_ref), channel_id=1, source_target_pairs={{2,16},{16,2},{3,17},{17,3},{6,20},{20,6},{7,21},{21,7},{10,24},{2... | collective-permute-start | bytes 786440 | tf_op jit(solution)/shard_map/ppermute | solution.py:289
  19.2 0.0 copy-done
  19.2 0.7 %shard_map.83 = (f32[8,256,256]{2,1,0:T(8,128)S(1)}, f32[8,256,256]{2,1,0:T(8,128)S(1)}) custom-call(bf16[1024,256]{1,0:T(8,128)(2,1)S(1)} %copy-done, bf16[256,128]{1,0:T(8,128)(2,1)S(1)} %get-tuple-element.60.refs_0_, bf16[256,128]{1,0:T(8,128)(2,1)S(1)} %get-tuple-element.61.refs_1_, bf16[256,128]{1,0:T(8,128)(2,1)S(1)} %get-tuple-element.62.refs_2_, ...), custom_call_target="tpu_custom_call" | custom-call | flops 536870912 | bytes 1572864 | tf_op jit(solution)/shard_map/pallas_call | solution.py:223
  20.0 0.0 collective-permute-done.5.halo_ref
  20.0 0.9 %shard_map.85 = bf16[256,128]{1,0:T(8,128)(2,1)S(1)} custom-call(s32[4]{0:T(128)S(1)} %pad_add_fusion.me_ref, bf16[2048,128]{1,0:T(8,128)(2,1)S(1)} %collective-permute-done.5.halo_ref, bf16[1024,256]{1,0:T(8,128)(2,1)S(1)} %copy-done, f32[8,256,256]{2,1,0:T(8,128)S(1)} %get-tuple-element.76.own_hat, f32[8,256,256]{2,1,0:T(8,128)S(1)} %get-tuple-element.77.taps_hat, ...), custom_call_target="tpu_custom_call" | custom-call | flops 268435456 | bytes 5308432 | tf_op jit(solution)/shard_map/pallas_call | solution.py:223
  20.9 3.1 %collective-permute-start.9 = (bf16[256,128]{1,0:T(8,128)(2,1)S(1)}, bf16[256,128]{1,0:T(8,128)(2,1)S(1)}, u32[]{:S(2)}, u32[]{:S(2)}) collective-permute-start(bf16[256,128]{1,0:T(8,128)(2,1)S(1)} %shard_map.85), channel_id=1, source_target_pairs={{0,8},{2,10},{4,12},{6,14},{8,0},{10,2},{12,4},{14,6},{1,9},{3,11}... | collective-permute-start | bytes 196616 | tf_op jit(solution)/shard_map/ppermute | solution.py:262
  23.9 2.2 %shard_map.84 = (bf16[256,128]{1,0:T(8,128)(2,1)S(1)}, bf16[256,128]{1,0:T(8,128)(2,1)S(1)}, bf16[256,128]{1,0:T(8,128)(2,1)S(1)}, bf16[256,128]{1,0:T(8,128)(2,...) custom-call(s32[4]{0:T(128)S(1)} %pad_add_fusion.me_ref, ...), custom_call_target="tpu_custom_call" | custom-call | flops 1610612736 | bytes 5701648 | tf_op jit(solution)/shard_map/pallas_call | solution.py:223
  26.2 1.4 %collective-permute-start.10 = (bf16[256,128]{1,0:T(8,128)(2,1)S(1)}, bf16[256,128]{1,0:T(8,128)(2,1)S(1)}, u32[]{:S(2)}, u32[]{:S(2)}) collective-permute-start(bf16[256,128]{1,0:T(8,128)(2,1)S(1)} %get-tuple-element.90), channel_id=1, source_target_pairs={{0,10},{2,8},{4,14},{6,12},{8,2},{10,0},{12,6},{14,4},{1,11},{3,9}... | collective-permute-start | bytes 196616 | tf_op jit(solution)/shard_map/ppermute | solution.py:262
  27.6 0.1 copy.9.skip_ref
  27.7 2.7 %collective-permute-start.11 = (bf16[256,128]{1,0:T(8,128)(2,1)S(1)}, bf16[256,128]{1,0:T(8,128)(2,1)S(1)}, u32[]{:S(2)}, u32[]{:S(2)}) collective-permute-start(bf16[256,128]{1,0:T(8,128)(2,1)S(1)} %get-tuple-element.91), channel_id=1, source_target_pairs={{0,12},{2,14},{4,8},{6,10},{8,4},{10,6},{12,0},{14,2},{1,13},{3,15... | collective-permute-start | bytes 196616 | tf_op jit(solution)/shard_map/ppermute | solution.py:262
  30.4 0.0 collective-permute-done.3.first_ref
  30.4 0.6 collective-permute-start.12
  31.0 0.0 collective-permute-done.4.second_ref
  31.0 0.7 %collective-permute-start.6 = (bf16[256,128]{1,0:T(8,128)(2,1)S(1)}, bf16[256,128]{1,0:T(8,128)(2,1)S(1)}, u32[]{:S(2)}, u32[]{:S(2)}) collective-permute-start(bf16[256,128]{1,0:T(8,128)(2,1)S(1)} %get-tuple-element.86), channel_id=1, source_target_pairs={{0,2},{2,0},{4,6},{6,4},{8,10},{10,8},{12,14},{14,12},{1,3},{3,1},... | collective-permute-start | bytes 196616 | tf_op jit(solution)/shard_map/ppermute | solution.py:262
  31.7 0.0 collective-permute-done.9.refs_4_
  31.7 0.0 collective-permute-start.7
  31.7 0.0 collective-permute-done.10.refs_5_
  31.7 1.4 %collective-permute-start.8 = (bf16[256,128]{1,0:T(8,128)(2,1)S(1)}, bf16[256,128]{1,0:T(8,128)(2,1)S(1)}, u32[]{:S(2)}, u32[]{:S(2)}) collective-permute-start(bf16[256,128]{1,0:T(8,128)(2,1)S(1)} %get-tuple-element.88), channel_id=1, source_target_pairs={{0,6},{2,4},{4,2},{6,0},{8,14},{10,12},{12,10},{14,8},{1,7},{3,5},... | collective-permute-start | bytes 196616 | tf_op jit(solution)/shard_map/ppermute | solution.py:262
  33.1 3.2 %shard_map.82.refs_8_.filt_ref = f32[8,256,256]{2,1,0:T(8,128)S(1)} custom-call(s32[4]{0:T(128)S(1)} %pad_add_fusion.me_ref, bf16[4,256,128]{2,1,0:T(8,128)(2,1)S(1)} %pad_maximum_fusion.held_ref, bf16[4,256,128]{2,1,0:T(8,128)(2,1)S(1)} %collective-permute-done.3.first_ref, bf16[4,256,128]{2,1,0:T(8,128)(2,1)S(1)} %collective-permute-done.4.second_ref, ...), custom_call_target="tpu_custom_call" | custom-call | flops 1610612736 | bytes 1377296 | tf_op jit(solution)/shard_map/pallas_call | solution.py:223
  36.3 0.0 collective-permute-done.11.refs_6_
  36.3 0.0 collective-permute-done.12.refs_7_
  36.3 0.0 collective-permute-done.6.refs_1_
  36.3 1.3 %collective-permute-done.7.refs_2_ = bf16[256,128]{1,0:T(8,128)(2,1)S(1)} collective-permute-done((bf16[256,128]{1,0:T(8,128)(2,1)S(1)}, bf16[256,128]{1,0:T(8,128)(2,1)S(1)}, u32[]{:S(2)}, u32[]{:S(2)}) %collective-permute-start.7) | collective-permute-done | bytes 65568 | tf_op jit(solution)/shard_map/ppermute | solution.py:262
  37.6 0.4 collective-permute-done.8.refs_3_
  38.0 1.9 %shard_map.86 = (bf16[256,128]{1,0:T(8,128)(2,1)S(1)}, f32[8,256,256]{2,1,0:T(8,128)S(1)}) custom-call(s32[4]{0:T(128)S(1)} %pad_add_fusion.me_ref, bf16[256,128]{1,0:T(8,128)(2,1)S(1)} %get-tuple-element.85.refs_0_, bf16[256,128]{1,0:T(8,128)(2,1)S(1)} %collective-permute-done.6.refs_1_, bf16[256,128]{1,0:T(8,128)(2,1)S(1)} %collective-permute-done.7.refs_2_, ...), custom_call_target="tpu_custom_call" | custom-call | flops 805306368 | bytes 3145744 | tf_op jit(solution)/shard_map/pallas_call | solution.py:223
  39.9 0.0 copy-start.1
  39.9 2.6 %shard_map.87 = (bf16[256,128]{1,0:T(8,128)(2,1)S(1)}, bf16[256,128]{1,0:T(8,128)(2,1)S(1)}, bf16[256,128]{1,0:T(8,128)(2,1)S(1)}, bf16[256,128]{1,0:T(8,128)(2,...) custom-call(s32[4]{0:T(128)S(1)} %pad_add_fusion.me_ref, ...), custom_call_target="tpu_custom_call" | custom-call | flops 805306368 | bytes 4718608 | tf_op jit(solution)/shard_map/pallas_call | solution.py:223
  42.5 2.1 %collective-permute-start.13 = (bf16[256,128]{1,0:T(8,128)(2,1)S(1)}, bf16[256,128]{1,0:T(8,128)(2,1)S(1)}, u32[]{:S(2)}, u32[]{:S(2)}) collective-permute-start(bf16[256,128]{1,0:T(8,128)(2,1)S(1)} %get-tuple-element.95), channel_id=1, source_target_pairs={{0,2},{2,0},{4,6},{6,4},{8,10},{10,8},{12,14},{14,12},{1,3},{3,1},... | collective-permute-start | bytes 196616 | tf_op jit(solution)/shard_map/ppermute | solution.py:262
  44.7 1.4 %collective-permute-start.14 = (bf16[256,128]{1,0:T(8,128)(2,1)S(1)}, bf16[256,128]{1,0:T(8,128)(2,1)S(1)}, u32[]{:S(2)}, u32[]{:S(2)}) collective-permute-start(bf16[256,128]{1,0:T(8,128)(2,1)S(1)} %get-tuple-element.96), channel_id=1, source_target_pairs={{0,6},{2,4},{4,2},{6,0},{8,14},{10,12},{12,10},{14,8},{1,7},{3,5},... | collective-permute-start | bytes 196616 | tf_op jit(solution)/shard_map/ppermute | solution.py:262
  46.0 0.4 collective-permute-start.15
  46.4 0.4 collective-permute-start.16
  46.8 3.1 %collective-permute-start.17 = (bf16[256,128]{1,0:T(8,128)(2,1)S(1)}, bf16[256,128]{1,0:T(8,128)(2,1)S(1)}, u32[]{:S(2)}, u32[]{:S(2)}) collective-permute-start(bf16[256,128]{1,0:T(8,128)(2,1)S(1)} %get-tuple-element.99), channel_id=1, source_target_pairs={{0,12},{2,14},{4,8},{6,10},{8,4},{10,6},{12,0},{14,2},{1,13},{3,15... | collective-permute-start | bytes 196616 | tf_op jit(solution)/shard_map/ppermute | solution.py:262
  49.9 0.0 collective-permute-done.13.refs_1_
  49.9 0.0 collective-permute-start.18
  50.0 0.0 collective-permute-done.14.refs_2_
  50.0 2.6 %collective-permute-start.19 = (bf16[256,128]{1,0:T(8,128)(2,1)S(1)}, bf16[256,128]{1,0:T(8,128)(2,1)S(1)}, u32[]{:S(2)}, u32[]{:S(2)}) collective-permute-start(bf16[256,128]{1,0:T(8,128)(2,1)S(1)} %get-tuple-element.101), channel_id=1, source_target_pairs={{0,8},{2,10},{4,12},{6,14},{8,0},{10,2},{12,4},{14,6},{1,9},{3,11}... | collective-permute-start | bytes 196616 | tf_op jit(solution)/shard_map/ppermute | solution.py:262
  52.6 0.0 copy-done.1
  52.6 0.0 collective-permute-done.15.refs_3_
  52.6 0.0 collective-permute-done.16.refs_4_
  52.6 1.8 %collective-permute-done.17.refs_5_ = bf16[256,128]{1,0:T(8,128)(2,1)S(1)} collective-permute-done((bf16[256,128]{1,0:T(8,128)(2,1)S(1)}, bf16[256,128]{1,0:T(8,128)(2,1)S(1)}, u32[]{:S(2)}, u32[]{:S(2)}) %collective-permute-start.17) | collective-permute-done | bytes 65568 | tf_op jit(solution)/shard_map/ppermute | solution.py:262
  54.4 5.9 %collective-permute-done.18.refs_6_ = bf16[256,128]{1,0:T(8,128)(2,1)S(1)} collective-permute-done((bf16[256,128]{1,0:T(8,128)(2,1)S(1)}, bf16[256,128]{1,0:T(8,128)(2,1)S(1)}, u32[]{:S(2)}, u32[]{:S(2)}) %collective-permute-start.18) | collective-permute-done | bytes 65568 | tf_op jit(solution)/shard_map/ppermute | solution.py:262
  60.3 1.4 %collective-permute-done.19.refs_7_ = bf16[256,128]{1,0:T(8,128)(2,1)S(1)} collective-permute-done((bf16[256,128]{1,0:T(8,128)(2,1)S(1)}, bf16[256,128]{1,0:T(8,128)(2,1)S(1)}, u32[]{:S(2)}, u32[]{:S(2)}) %collective-permute-start.19) | collective-permute-done | bytes 65568 | tf_op jit(solution)/shard_map/ppermute | solution.py:262
  61.6 1.4 %shard_map.88 = bf16[2048,128]{1,0:T(8,128)(2,1)} custom-call(s32[4]{0:T(128)S(1)} %pad_add_fusion.me_ref, bf16[256,128]{1,0:T(8,128)(2,1)S(1)} %get-tuple-element.94.refs_0_, bf16[256,128]{1,0:T(8,128)(2,1)S(1)} %collective-permute-done.13.refs_1_, bf16[256,128]{1,0:T(8,128)(2,1)S(1)} %collective-permute-done.14.refs_2_, ...), custom_call_target="tpu_custom_call" | custom-call | flops 262144 | bytes 1048592 | tf_op jit(solution)/shard_map/pallas_call | solution.py:223
  (2 shorter events, 0.1 us)
Async XLA Ops:
  0.0 5.6 %copy-start.2 = (bf16[2048,128]{1,0:T(8,128)(2,1)S(1)}, bf16[2048,128]{1,0:T(8,128)(2,1)}, u32[]{:S(2)}) copy-start(bf16[2048,128]{1,0:T(8,128)(2,1)} %param.10) | copy-start | bytes 1572868
  0.0 5.6 %copy-start.3 = (bf16[2048,128]{1,0:T(8,128)(2,1)S(1)}, bf16[2048,128]{1,0:T(8,128)(2,1)}, u32[]{:S(2)}) copy-start(bf16[2048,128]{1,0:T(8,128)(2,1)} %param.9) | copy-start | bytes 1572868
  0.0 20.0 %collective-permute-start.5 = (bf16[2048,128]{1,0:T(8,128)(2,1)}, bf16[2048,128]{1,0:T(8,128)(2,1)S(1)}, u32[]{:S(2)}, u32[]{:S(2)}) collective-permute-start(bf16[2048,128]{1,0:T(8,128)(2,1)} %param.8), channel_id=1, source_target_pairs={{0,2},{2,4},{4,6},{6,8},{8,10},{10,12},{12,14},{1,3},{3,5},{5,7},{... | collective-permute-start | bytes 1572872 | tf_op jit(solution)/shard_map/ppermute | solution.py:264
  3.4 15.8 %copy-start = (bf16[1024,256]{1,0:T(8,128)(2,1)S(1)}, bf16[1024,256]{1,0:T(8,128)(2,1)}, u32[]{:S(2)}) copy-start(bf16[1024,256]{1,0:T(8,128)(2,1)} %constant.35.clone.table_ref.refs_9_) | copy-start | bytes 1572868
  5.7 5.3 %collective-permute-start = (bf16[256,128]{1,0:T(8,128)(2,1)S(1)}, bf16[256,128]{1,0:T(8,128)(2,1)S(1)}, u32[]{:S(2)}, u32[]{:S(2)}) collective-permute-start(bf16[256,128]{1,0:T(8,128)(2,1)S(1)} %get-tuple-element.55), channel_id=1, source_target_pairs={{0,4},{4,0},{8,12},{12,8},{1,5},{5,1},{9,13},{13,9},{2,6},{6,2},{1... | collective-permute-start | bytes 196616 | tf_op jit(solution)/shard_map/ppermute | solution.py:280
  8.3 7.6 %collective-permute-start.1 = (bf16[256,128]{1,0:T(8,128)(2,1)S(1)}, bf16[256,128]{1,0:T(8,128)(2,1)S(1)}, u32[]{:S(2)}, u32[]{:S(2)}) collective-permute-start(bf16[256,128]{1,0:T(8,128)(2,1)S(1)} %get-tuple-element.56), channel_id=1, source_target_pairs={{0,8},{4,12},{8,0},{12,4},{1,9},{5,13},{9,1},{13,5},{2,10},{6,14},... | collective-permute-start | bytes 196616 | tf_op jit(solution)/shard_map/ppermute | solution.py:280
  10.9 6.1 %collective-permute-start.2 = (bf16[256,128]{1,0:T(8,128)(2,1)S(1)}, bf16[256,128]{1,0:T(8,128)(2,1)S(1)}, u32[]{:S(2)}, u32[]{:S(2)}) collective-permute-start(bf16[256,128]{1,0:T(8,128)(2,1)S(1)} %get-tuple-element.57), channel_id=1, source_target_pairs={{0,12},{4,8},{8,4},{12,0},{1,13},{5,9},{9,5},{13,1},{2,14},{6,10},... | collective-permute-start | bytes 196616 | tf_op jit(solution)/shard_map/ppermute | solution.py:280
  17.0 13.4 %collective-permute-start.3 = (bf16[4,256,128]{2,1,0:T(8,128)(2,1)S(1)}, bf16[4,256,128]{2,1,0:T(8,128)(2,1)S(1)}, u32[]{:S(2)}, u32[]{:S(2)}) collective-permute-start(bf16[4,256,128]{2,1,0:T(8,128)(2,1)S(1)} %pad_maximum_fusion.held_ref), channel_id=1, source_target_pairs={{0,16},{18,2},{2,0},{16,18},{1,17},{19,3},{3,1},{17,19},{4,20},{22... | collective-permute-start | bytes 786440 | tf_op jit(solution)/shard_map/ppermute | solution.py:288
  18.6 12.5 %collective-permute-start.4 = (bf16[4,256,128]{2,1,0:T(8,128)(2,1)S(1)}, bf16[4,256,128]{2,1,0:T(8,128)(2,1)S(1)}, u32[]{:S(2)}, u32[]{:S(2)}) collective-permute-start(bf16[4,256,128]{2,1,0:T(8,128)(2,1)S(1)} %pad_maximum_fusion.held_ref), channel_id=1, source_target_pairs={{2,16},{16,2},{3,17},{17,3},{6,20},{20,6},{7,21},{21,7},{10,24},{2... | collective-permute-start | bytes 786440 | tf_op jit(solution)/shard_map/ppermute | solution.py:289
  20.9 10.8 %collective-permute-start.9 = (bf16[256,128]{1,0:T(8,128)(2,1)S(1)}, bf16[256,128]{1,0:T(8,128)(2,1)S(1)}, u32[]{:S(2)}, u32[]{:S(2)}) collective-permute-start(bf16[256,128]{1,0:T(8,128)(2,1)S(1)} %shard_map.85), channel_id=1, source_target_pairs={{0,8},{2,10},{4,12},{6,14},{8,0},{10,2},{12,4},{14,6},{1,9},{3,11}... | collective-permute-start | bytes 196616 | tf_op jit(solution)/shard_map/ppermute | solution.py:262
  26.2 5.6 %collective-permute-start.10 = (bf16[256,128]{1,0:T(8,128)(2,1)S(1)}, bf16[256,128]{1,0:T(8,128)(2,1)S(1)}, u32[]{:S(2)}, u32[]{:S(2)}) collective-permute-start(bf16[256,128]{1,0:T(8,128)(2,1)S(1)} %get-tuple-element.90), channel_id=1, source_target_pairs={{0,10},{2,8},{4,14},{6,12},{8,2},{10,0},{12,6},{14,4},{1,11},{3,9}... | collective-permute-start | bytes 196616 | tf_op jit(solution)/shard_map/ppermute | solution.py:262
  27.7 8.6 %collective-permute-start.11 = (bf16[256,128]{1,0:T(8,128)(2,1)S(1)}, bf16[256,128]{1,0:T(8,128)(2,1)S(1)}, u32[]{:S(2)}, u32[]{:S(2)}) collective-permute-start(bf16[256,128]{1,0:T(8,128)(2,1)S(1)} %get-tuple-element.91), channel_id=1, source_target_pairs={{0,12},{2,14},{4,8},{6,10},{8,4},{10,6},{12,0},{14,2},{1,13},{3,15... | collective-permute-start | bytes 196616 | tf_op jit(solution)/shard_map/ppermute | solution.py:262
  30.4 5.9 %collective-permute-start.12 = (bf16[256,128]{1,0:T(8,128)(2,1)S(1)}, bf16[256,128]{1,0:T(8,128)(2,1)S(1)}, u32[]{:S(2)}, u32[]{:S(2)}) collective-permute-start(bf16[256,128]{1,0:T(8,128)(2,1)S(1)} %get-tuple-element.92), channel_id=1, source_target_pairs={{0,14},{2,12},{4,10},{6,8},{8,6},{10,4},{12,2},{14,0},{1,15},{3,13... | collective-permute-start | bytes 196616 | tf_op jit(solution)/shard_map/ppermute | solution.py:262
  31.0 5.3 %collective-permute-start.6 = (bf16[256,128]{1,0:T(8,128)(2,1)S(1)}, bf16[256,128]{1,0:T(8,128)(2,1)S(1)}, u32[]{:S(2)}, u32[]{:S(2)}) collective-permute-start(bf16[256,128]{1,0:T(8,128)(2,1)S(1)} %get-tuple-element.86), channel_id=1, source_target_pairs={{0,2},{2,0},{4,6},{6,4},{8,10},{10,8},{12,14},{14,12},{1,3},{3,1},... | collective-permute-start | bytes 196616 | tf_op jit(solution)/shard_map/ppermute | solution.py:262
  31.7 5.9 %collective-permute-start.7 = (bf16[256,128]{1,0:T(8,128)(2,1)S(1)}, bf16[256,128]{1,0:T(8,128)(2,1)S(1)}, u32[]{:S(2)}, u32[]{:S(2)}) collective-permute-start(bf16[256,128]{1,0:T(8,128)(2,1)S(1)} %get-tuple-element.87), channel_id=1, source_target_pairs={{0,4},{2,6},{4,0},{6,2},{8,12},{10,14},{12,8},{14,10},{1,5},{3,7},... | collective-permute-start | bytes 196616 | tf_op jit(solution)/shard_map/ppermute | solution.py:262
  31.7 6.3 %collective-permute-start.8 = (bf16[256,128]{1,0:T(8,128)(2,1)S(1)}, bf16[256,128]{1,0:T(8,128)(2,1)S(1)}, u32[]{:S(2)}, u32[]{:S(2)}) collective-permute-start(bf16[256,128]{1,0:T(8,128)(2,1)S(1)} %get-tuple-element.88), channel_id=1, source_target_pairs={{0,6},{2,4},{4,2},{6,0},{8,14},{10,12},{12,10},{14,8},{1,7},{3,5},... | collective-permute-start | bytes 196616 | tf_op jit(solution)/shard_map/ppermute | solution.py:262
  39.9 12.6 %copy-start.1 = (bf16[2048,128]{1,0:T(8,128)(2,1)S(1)}, bf16[2048,128]{1,0:T(8,128)(2,1)}, u32[]{:S(2)}) copy-start(bf16[2048,128]{1,0:T(8,128)(2,1)} %param.14) | copy-start | bytes 1572868
  42.5 7.4 %collective-permute-start.13 = (bf16[256,128]{1,0:T(8,128)(2,1)S(1)}, bf16[256,128]{1,0:T(8,128)(2,1)S(1)}, u32[]{:S(2)}, u32[]{:S(2)}) collective-permute-start(bf16[256,128]{1,0:T(8,128)(2,1)S(1)} %get-tuple-element.95), channel_id=1, source_target_pairs={{0,2},{2,0},{4,6},{6,4},{8,10},{10,8},{12,14},{14,12},{1,3},{3,1},... | collective-permute-start | bytes 196616 | tf_op jit(solution)/shard_map/ppermute | solution.py:262
  44.7 5.3 %collective-permute-start.14 = (bf16[256,128]{1,0:T(8,128)(2,1)S(1)}, bf16[256,128]{1,0:T(8,128)(2,1)S(1)}, u32[]{:S(2)}, u32[]{:S(2)}) collective-permute-start(bf16[256,128]{1,0:T(8,128)(2,1)S(1)} %get-tuple-element.96), channel_id=1, source_target_pairs={{0,6},{2,4},{4,2},{6,0},{8,14},{10,12},{12,10},{14,8},{1,7},{3,5},... | collective-permute-start | bytes 196616 | tf_op jit(solution)/shard_map/ppermute | solution.py:262
  46.0 6.6 %collective-permute-start.15 = (bf16[256,128]{1,0:T(8,128)(2,1)S(1)}, bf16[256,128]{1,0:T(8,128)(2,1)S(1)}, u32[]{:S(2)}, u32[]{:S(2)}) collective-permute-start(bf16[256,128]{1,0:T(8,128)(2,1)S(1)} %get-tuple-element.97), channel_id=1, source_target_pairs={{0,4},{2,6},{4,0},{6,2},{8,12},{10,14},{12,8},{14,10},{1,5},{3,7},... | collective-permute-start | bytes 196616 | tf_op jit(solution)/shard_map/ppermute | solution.py:262
  46.4 6.3 %collective-permute-start.16 = (bf16[256,128]{1,0:T(8,128)(2,1)S(1)}, bf16[256,128]{1,0:T(8,128)(2,1)S(1)}, u32[]{:S(2)}, u32[]{:S(2)}) collective-permute-start(bf16[256,128]{1,0:T(8,128)(2,1)S(1)} %get-tuple-element.98), channel_id=1, source_target_pairs={{0,14},{2,12},{4,10},{6,8},{8,6},{10,4},{12,2},{14,0},{1,15},{3,13... | collective-permute-start | bytes 196616 | tf_op jit(solution)/shard_map/ppermute | solution.py:262
  46.8 7.6 %collective-permute-start.17 = (bf16[256,128]{1,0:T(8,128)(2,1)S(1)}, bf16[256,128]{1,0:T(8,128)(2,1)S(1)}, u32[]{:S(2)}, u32[]{:S(2)}) collective-permute-start(bf16[256,128]{1,0:T(8,128)(2,1)S(1)} %get-tuple-element.99), channel_id=1, source_target_pairs={{0,12},{2,14},{4,8},{6,10},{8,4},{10,6},{12,0},{14,2},{1,13},{3,15... | collective-permute-start | bytes 196616 | tf_op jit(solution)/shard_map/ppermute | solution.py:262
  49.9 10.3 %collective-permute-start.18 = (bf16[256,128]{1,0:T(8,128)(2,1)S(1)}, bf16[256,128]{1,0:T(8,128)(2,1)S(1)}, u32[]{:S(2)}, u32[]{:S(2)}) collective-permute-start(bf16[256,128]{1,0:T(8,128)(2,1)S(1)} %get-tuple-element.100), channel_id=1, source_target_pairs={{0,10},{2,8},{4,14},{6,12},{8,2},{10,0},{12,6},{14,4},{1,11},{3,9}... | collective-permute-start | bytes 196616 | tf_op jit(solution)/shard_map/ppermute | solution.py:262
  50.0 11.7 %collective-permute-start.19 = (bf16[256,128]{1,0:T(8,128)(2,1)S(1)}, bf16[256,128]{1,0:T(8,128)(2,1)S(1)}, u32[]{:S(2)}, u32[]{:S(2)}) collective-permute-start(bf16[256,128]{1,0:T(8,128)(2,1)S(1)} %get-tuple-element.101), channel_id=1, source_target_pairs={{0,8},{2,10},{4,12},{6,14},{8,0},{10,2},{12,4},{14,6},{1,9},{3,11}... | collective-permute-start | bytes 196616 | tf_op jit(solution)/shard_map/ppermute | solution.py:262
